TPU v7x, 512 devices: a whole 4x8x8 slice. The times are simulated.
512 devices in a mesh: img: 16 (over z, core), ori: 32 (over x, y).
Axes of the slice: x: 4, y: 8, z: 8, core: 2. Of those that a mesh axis runs over, the one named last changes fastest.
Arguments:
- images: bfloat16 [1024, 16384], P(('img', 'ori')), may hold values from -8 to 8
- references: bfloat16 [512, 16384], P('ori'), may hold values from -6 to 6
- shifts: float32 [12, 2], replicated, may hold values from -3 to 3
- owners: int32 [65536, 1], P(('ori', 'img')), may hold values from 0 to 31; in each aligned block of 128 rows (0 to 127, 128 to 255, ...) at most 16 rows name the same one
- slot_rows: int32 [65536], P(('ori', 'img')), may hold values from 0 to 63
- interpolation: float32 [65536, 128], P(('ori', 'img')), may hold values from -0.5 to 0.5
- regularizer: float32 [32768], P(('ori', 'img')), may hold values from 1 to 16
Outputs:
- volume: float32 [32768, 128], P(('ori', 'img'))
- resampled: float32 [512, 16384], P(('ori', 'img'))
Inputs may be any that keep to these rules, and one draw needn't show every extreme that they name: `owners`: among the 128 segments of one device (aligned blocks of rows), no owner is named more than 16 times, a bound that some block reaches.
All inputs are finite; a program needn't handle non-finite values.
Results may differ from a plain program's by a relative error of at most 0.014.
Values may be sent and summed in bfloat16 or wider, within the bound.
A program may use at most 64 MiB of HBM per device.

v0:
```python
import math

import jax
import jax.numpy as jnp
from jax import lax
from jax.sharding import PartitionSpec as P

COEF = 16384
SEGLEN = 128
SHIFTS = 12
SEGS = 128


grid_width = 64
image_side = 128.0


def phase_tables(shifts):
    half_len = COEF // 2
    positions = jnp.arange(half_len, dtype=jnp.int32)
    freq_x = (positions % grid_width).astype(jnp.float32)
    freq_y = (positions // grid_width - half_len // grid_width // 2).astype(jnp.float32)
    angles = (
        2.0
        * math.pi
        / image_side
        * (shifts[:, 0:1] * freq_x[None, :] + shifts[:, 1:2] * freq_y[None, :])
    )
    return (jnp.cos(angles), jnp.sin(angles))


def one_rotation(real_part, imag_part, cosine_row, sine_row):
    rotated_re = real_part * cosine_row[None, :] - imag_part * sine_row[None, :]
    rotated_im = real_part * sine_row[None, :] + imag_part * cosine_row[None, :]
    return jnp.concatenate([rotated_re, rotated_im], axis=1).astype(jnp.bfloat16)


def backproject(weights_b, group_images, cosine_table, sine_table):
    half_len = COEF // 2
    orient_count = weights_b.shape[1]
    total_re = jnp.zeros((orient_count, half_len), jnp.float32)
    total_im = jnp.zeros((orient_count, half_len), jnp.float32)
    for shift_number in range(SHIFTS):
        summed = lax.dot_general(
            weights_b[:, :, shift_number],
            group_images,
            (((0,), (0,)), ((), ())),
            preferred_element_type=jnp.float32,
        )
        sum_re = summed[:, :half_len]
        sum_im = summed[:, half_len:]
        total_re = (
            total_re + sum_re * cosine_table[shift_number] + sum_im * sine_table[shift_number]
        )
        total_im = (
            total_im - sum_re * sine_table[shift_number] + sum_im * cosine_table[shift_number]
        )
    return jnp.concatenate([total_re, total_im], axis=1)


def shards(images, references, shifts, owners, slot_rows, interpolation, regularizer):
    cosine_table, sine_table = phase_tables(shifts)
    score_scale = 2.0 / math.sqrt(COEF)
    half_len = COEF // 2
    real_part = references[:, :half_len].astype(jnp.float32)
    imag_part = references[:, half_len:].astype(jnp.float32)
    group_images = lax.all_gather(images, "ori", axis=0, tiled=True)
    group_rows = group_images.shape[0]
    score_list = []
    for shift_number in range(SHIFTS):
        rotated = one_rotation(
            real_part, imag_part, cosine_table[shift_number], sine_table[shift_number]
        )
        score_list.append(
            lax.dot_general(
                group_images, rotated, (((1,), (1,)), ((), ())), preferred_element_type=jnp.float32
            )
        )
    scores = jnp.stack(score_list, axis=2).reshape(group_rows, -1) * score_scale
    row_peak = lax.pmax(jnp.max(scores, axis=1), "ori")
    exponent = jnp.exp(scores - row_peak[:, None])
    row_total = lax.psum(jnp.sum(exponent, axis=1), "ori")
    weights = exponent / row_total[:, None]
    orient_count = references.shape[0]
    weights3 = weights.reshape(group_rows, orient_count, SHIFTS)
    orient_mass = jnp.sum(weights3, axis=(0, 2))
    summed = backproject(weights3.astype(jnp.bfloat16), group_images, cosine_table, sine_table)
    sub_rows = orient_count // lax.axis_size("img")
    full_slices, full_mass = lax.psum((summed, orient_mass), "img")
    first_row = lax.axis_index("img") * sub_rows
    own_slices = lax.dynamic_slice_in_dim(full_slices, first_row, sub_rows, 0)
    own_mass = lax.dynamic_slice_in_dim(full_mass, first_row, sub_rows, 0)
    ori_count = lax.axis_size("ori")
    segments = own_slices.reshape(-1, SEGLEN)
    seg_count = segments.shape[0]
    seg_mass = jnp.repeat(own_mass, SEGS)
    capacity = max(2, 4 * seg_count // ori_count)
    dest_owner = owners[:, 0]
    onehot = (dest_owner[:, None] == jnp.arange(ori_count, dtype=jnp.int32)[None, :]).astype(
        jnp.int32
    )
    slot_rank = jnp.sum(jnp.cumsum(onehot, axis=0) * onehot, axis=1) - 1
    slot_index = dest_owner * capacity + slot_rank
    send_values = (
        jnp.zeros((ori_count * capacity, SEGLEN), jnp.float32).at[slot_index].set(segments)
    )
    send_mass = jnp.zeros((ori_count * capacity,), jnp.float32).at[slot_index].set(seg_mass)
    send_rows = (
        jnp.zeros((ori_count * capacity,), jnp.float32)
        .at[slot_index]
        .set(slot_rows.astype(jnp.float32))
    )
    got_values, got_mass, got_rows = (
        lax.all_to_all(
            send_values.reshape(ori_count, capacity, SEGLEN),
            "ori",
            split_axis=0,
            concat_axis=0,
            tiled=True,
        ),
        lax.all_to_all(
            send_mass.reshape(ori_count, capacity), "ori", split_axis=0, concat_axis=0, tiled=True
        ),
        lax.all_to_all(
            send_rows.reshape(ori_count, capacity), "ori", split_axis=0, concat_axis=0, tiled=True
        ),
    )
    flat_values = got_values.reshape(-1, SEGLEN)
    flat_rows = got_rows.reshape(-1).astype(jnp.int32)
    row_count = regularizer.shape[0]
    inserted = jnp.zeros((row_count, SEGLEN), jnp.float32).at[flat_rows].add(flat_values)
    weight_sum = jnp.zeros((row_count,), jnp.float32).at[flat_rows].add(got_mass.reshape(-1))
    mapped = jnp.dot(
        inserted, interpolation, precision=lax.Precision.HIGHEST, preferred_element_type=jnp.float32
    )
    volume = mapped / (weight_sum + regularizer)[:, None]
    back_values = lax.dot_general(
        volume,
        interpolation,
        (((1,), (1,)), ((), ())),
        precision=lax.Precision.HIGHEST,
        preferred_element_type=jnp.float32,
    )
    reply_values = back_values[flat_rows].reshape(ori_count, capacity, SEGLEN)
    returned = lax.all_to_all(reply_values, "ori", split_axis=0, concat_axis=0, tiled=True)
    resampled = returned.reshape(-1, SEGLEN)[slot_index].reshape(own_slices.shape)
    return (volume, resampled)


def solution(mesh):
    in_specs = (
        P(("img", "ori"), None),
        P("ori", None),
        P(),
        P(("ori", "img"), None),
        P(("ori", "img")),
        P(("ori", "img"), None),
        P(("ori", "img")),
    )
    out_specs = (P(("ori", "img"), None), P(("ori", "img"), None))
    return jax.shard_map(shards, mesh=mesh, in_specs=in_specs, out_specs=out_specs, check_vma=False)
```

profile of v0, /device:TPU:8, one launch (start us, length us, event | category | flops | bytes accessed | tf_op | source)
XLA Modules:
  0.0 433.6 jit_solution(10598141318772497419)
XLA Ops:
  8.7 1.9 fusion.97
  11.5 1.4 fusion.21
  13.0 1.4 fusion.33
  14.6 1.4 fusion.45
  17.2 81.1 %all-gather.3.cloned.1.call-done = bf16[32,2,16384]{2,1,0:T(2,128)(2,1)} async-done(((bf16[1,2,16384]{2,1,0:T(2,128)(2,1)}), bf16[32,2,16384]{2,1,0:T(2,128)(2,1)}) %all-gather.3.cloned.1.call-update) | async-done | bytes 2097168 | tf_op jit(solution)/shard_map/all_gather | solution.py:67
  98.2 2.7 reshape.178
  101.0 1.8 fusion.11
  111.2 71.1 %pmax.7 = f32[64]{0:T(128)S(1)} all-reduce(f32[64]{0:T(128)S(1)} %multiply_reduce_fusion), channel_id=1, replica_groups=mesh['img'=16,'ori'=32] {'ori'}, use_global_device_ids=true, to_apply=%region_4.5 | all-reduce | flops 64 | bytes 512 | tf_op jit(solution)/shard_map/pmax | solution.py:80
  183.2 71.8 %psum.21 = f32[64]{0:T(128)S(1)} all-reduce(f32[64]{0:T(128)S(1)} %fusion.101), channel_id=1, replica_groups=mesh['img'=16,'ori'=32] {'ori'}, use_global_device_ids=true, to_apply=%region_6.7 | all-reduce | flops 64 | bytes 512 | tf_op jit(solution)/shard_map/psum | solution.py:82
  261.5 1.4 multiply_add_fusion.1
  262.9 1.4 multiply_add_fusion
  267.6 3.6 all-to-all-start
  271.2 24.5 %psum.23 = f32[16]{0:T(128)S(1)} all-reduce(f32[16]{0:T(128)S(1)} %get-tuple-element.66), channel_id=1, replica_groups=mesh['img'=16,'ori'=32] {'img'}, use_global_device_ids=true, to_apply=%region_11.12 | all-reduce | flops 16 | bytes 128 | tf_op jit(solution)/shard_map/psum | solution.py:89
  298.6 9.5 %all-to-all-start.2 = ((f32[32,1,16]{2,1,0:T(1,128)}), f32[32,1,16]{2,1,0:T(1,128)S(1)}, u32[]{:S(2)}, u32[]{:S(2)}) async-start(f32[32,1,16]{2,1,0:T(1,128)} %bitcast.72), calls=%async_computation.2 | async-start | bytes 32768 | tf_op jit(solution)/shard_map/all_to_all | solution.py:121
  308.1 71.1 %all-reduce.2.cloned.1.call-done = f32[16,16384]{1,0:T(8,128)} async-done(((f32[16,16384]{1,0:T(8,128)}), f32[16,16384]{1,0:T(8,128)}) %all-reduce.2.cloned.1.call-update) | async-done | bytes 1048592 | tf_op jit(solution)/shard_map/psum | solution.py:89
  380.3 1.6 scatter_custom_fusion.1
  381.9 9.8 %all-to-all-start.1 = ((f32[32,16,128]{2,1,0:T(8,128)}), f32[32,16,128]{2,1,0:T(8,128)S(1)}, u32[]{:S(2)}, u32[]{:S(2)}) async-start(f32[32,16,128]{2,1,0:T(8,128)} %bitcast.69), calls=%async_computation.1 | async-start | bytes 524288 | tf_op jit(solution)/shard_map/all_to_all | solution.py:114
  393.2 4.3 scatter_fusion
  397.5 6.4 %all-to-all-done.1 = f32[32,16,128]{2,1,0:T(8,128)S(1)} async-done(((f32[32,16,128]{2,1,0:T(8,128)}), f32[32,16,128]{2,1,0:T(8,128)S(1)}, u32[]{:S(2)}, u32[]{:S(2)}) %all-to-all-start.1) | async-done | bytes 262176 | tf_op jit(solution)/shard_map/all_to_all | solution.py:114
  403.9 3.7 scatter_custom_fusion.2
  408.0 1.7 gather_fusion
  409.7 4.6 %all-to-all-start.3 = ((f32[32,16,128]{2,1,0:T(8,128)}), f32[32,16,128]{2,1,0:T(8,128)S(1)}, u32[]{:S(2)}, u32[]{:S(2)}) async-start(f32[32,16,128]{2,1,0:T(8,128)} %bitcast.73), calls=%async_computation.3 | async-start | bytes 524288 | tf_op jit(solution)/shard_map/all_to_all | solution.py:145
  414.3 11.3 %all-to-all-done.3 = f32[32,16,128]{2,1,0:T(8,128)S(1)} async-done(((f32[32,16,128]{2,1,0:T(8,128)}), f32[32,16,128]{2,1,0:T(8,128)S(1)}, u32[]{:S(2)}, u32[]{:S(2)}) %all-to-all-start.3) | async-done | bytes 262176 | tf_op jit(solution)/shard_map/all_to_all | solution.py:145
  425.5 1.2 gather_fusion.1
  (196 shorter events, 28.1 us)
Async XLA Ops:
  7.2 400.4 %copy-start = (f32[128,128]{1,0:T(8,128)S(1)}, f32[128,128]{1,0:T(8,128)}, u32[]{:S(2)}) copy-start(f32[128,128]{1,0:T(8,128)} %param.12) | copy-start | bytes 196612
  7.2 4.3 %copy-start.2 = (bf16[16,16384]{1,0:T(8,128)(2,1)S(1)}, bf16[16,16384]{1,0:T(8,128)(2,1)}, u32[]{:S(2)}) copy-start(bf16[16,16384]{1,0:T(8,128)(2,1)} %param.8) | copy-start | bytes 1572868
  7.2 91.1 %all-gather.3.cloned.1.call-start = ((), (), s32[]{:S(2)}) async-start(), calls=%async_computation.5 | async-start | bytes 2162688 | tf_op jit(solution)/shard_map/all_gather | solution.py:67
  7.9 371.3 %all-reduce.2.cloned.1.call-start = ((), (), s32[]{:S(2)}) async-start(), calls=%async_computation.4 | async-start | bytes 2097152 | tf_op jit(solution)/shard_map/psum | solution.py:89
  11.0 3.4 copy-start.29
  11.0 3.4 copy-start.31
  11.0 3.4 copy-start.33
  11.0 3.4 copy-start.35
  11.0 3.4 copy-start.37
  11.0 3.4 copy-start.39
  11.1 3.5 copy-start.23
  11.1 3.5 copy-start.25
  11.1 3.5 copy-start.27
  11.1 4.9 %copy-start.21 = (f32[1,8192]{1,0:T(1,128)}, f32[1,8192]{1,0:T(1,128)S(1)}, u32[]{:S(2)}) copy-start(f32[1,8192]{1,0:T(1,128)S(1)} %get-tuple-element.32) | copy-start | bytes 98308
  11.5 3.1 copy-start.47
  11.5 4.5 %copy-start.41 = (f32[1,8192]{1,0:T(1,128)}, f32[1,8192]{1,0:T(1,128)S(1)}, u32[]{:S(2)}) copy-start(f32[1,8192]{1,0:T(1,128)S(1)} %get-tuple-element.42) | copy-start | bytes 98308
  11.5 4.5 %copy-start.43 = (f32[1,8192]{1,0:T(1,128)}, f32[1,8192]{1,0:T(1,128)S(1)}, u32[]{:S(2)}) copy-start(f32[1,8192]{1,0:T(1,128)S(1)} %get-tuple-element.43) | copy-start | bytes 98308
  11.5 4.5 %copy-start.45 = (f32[1,8192]{1,0:T(1,128)}, f32[1,8192]{1,0:T(1,128)S(1)}, u32[]{:S(2)}) copy-start(f32[1,8192]{1,0:T(1,128)S(1)} %get-tuple-element.44) | copy-start | bytes 98308
  264.4 128.8 %copy-start.1 = (f32[64]{0:T(128)S(1)}, f32[64]{0:T(128)}, u32[]{:S(2)}) copy-start(f32[64]{0:T(128)} %param.13) | copy-start | bytes 772
  267.6 31.0 %all-to-all-start = ((f32[32,1,16]{2,1,0:T(1,128)}), f32[32,1,16]{2,1,0:T(1,128)S(1)}, u32[]{:S(2)}, u32[]{:S(2)}) async-start(f32[32,1,16]{2,1,0:T(1,128)} %bitcast.3), calls=%async_computation | async-start | bytes 32768 | tf_op jit(solution)/shard_map/all_to_all | solution.py:124
  298.6 83.2 %all-to-all-start.2 = ((f32[32,1,16]{2,1,0:T(1,128)}), f32[32,1,16]{2,1,0:T(1,128)S(1)}, u32[]{:S(2)}, u32[]{:S(2)}) async-start(f32[32,1,16]{2,1,0:T(1,128)} %bitcast.72), calls=%async_computation.2 | async-start | bytes 32768 | tf_op jit(solution)/shard_map/all_to_all | solution.py:121
  381.9 22.0 %all-to-all-start.1 = ((f32[32,16,128]{2,1,0:T(8,128)}), f32[32,16,128]{2,1,0:T(8,128)S(1)}, u32[]{:S(2)}, u32[]{:S(2)}) async-start(f32[32,16,128]{2,1,0:T(8,128)} %bitcast.69), calls=%async_computation.1 | async-start | bytes 524288 | tf_op jit(solution)/shard_map/all_to_all | solution.py:114
  407.8 19.0 %copy-start.65 = (f32[64,128]{1,0:T(8,128)}, f32[64,128]{1,0:T(8,128)S(1)}, u32[]{:S(2)}) copy-start(f32[64,128]{1,0:T(8,128)S(1)} %convolution_divide_fusion) | copy-start | bytes 98308
  409.7 15.9 %all-to-all-start.3 = ((f32[32,16,128]{2,1,0:T(8,128)}), f32[32,16,128]{2,1,0:T(8,128)S(1)}, u32[]{:S(2)}, u32[]{:S(2)}) async-start(f32[32,16,128]{2,1,0:T(8,128)} %bitcast.73), calls=%async_computation.3 | async-start | bytes 524288 | tf_op jit(solution)/shard_map/all_to_all | solution.py:145
  (50 other events, 74.9 us)
Sparse Core Ops, SparseCore 0:
  11.2 87.0 all-gather.2
  265.6 113.5 all-reduce.1
where the time goes:
time: 434 us
  waiting for transfers between devices  171 us (39%)
  blocking collectives  167 us (38%)
  starting transfers between devices  27.6 us (6%)
  other arithmetic  22.4 us (5%)
  local copies, waits for them, and re-layouts  16.4 us (4%)
  between operations  15 us (3%)
  matrix products  14.4 us (3%)
    all_gather x1, waiting for transfers between devices, shards(): group_images = lax.all_gather(images, 'ori', axis=0, tiled=True)  81.1 us
    psum x1, blocking collectives, shards(): row_total = lax.psum(jnp.sum(exponent, axis=1), 'ori')  71.8 us
    psum x1, waiting for transfers between devices, shards(): full_slices, full_mass = lax.psum((summed, orient_mass), 'img')  71.1 us
    pmax x1, blocking collectives, shards(): row_peak = lax.pmax(jnp.max(scores, axis=1), 'ori')  71.1 us
    psum x1, blocking collectives, shards(): full_slices, full_mass = lax.psum((summed, orient_mass), 'img')  24.5 us
    all_to_all x1, waiting for transfers between devices, shards(): lax.all_to_all(reply_values, 'ori', split_axis=0, concat_axis=0, tiled=True)  11.3 us
    all_to_all x1, starting transfers between devices, shards(): lax.all_to_all(send_values.reshape(ori_count, capacity, SEGLEN), 'ori', s...  9.85 us
    all_to_all x1, starting transfers between devices, shards(): lax.all_to_all(send_mass.reshape(ori_count, capacity), 'ori', split_axis=...  9.49 us
  transfers between devices with their start and end apart: 6, of which 4 were waited for; matrix products, arithmetic and copies ran while one was open for 5% of the time, Pallas kernels for 0%

commit v1 on v0

v1 whole, which is shorter than its diff:
```python
import heapq
import math

import jax
import jax.numpy as jnp
from jax import lax
from jax.experimental import pallas as pl
from jax.experimental.pallas import tpu as pltpu
from jax.sharding import PartitionSpec as P

NX, NY, NZ = 4, 8, 8
N_ORI = NX * NY
N_IMG = 2 * NZ
COEF = 16384
QUART = COEF // 4
SHIFTS = 12
CAP = 16
SLOTS = N_ORI * CAP
ROWS = 64
MESH = pl.DeviceIdType.MESH
HIGH = lax.Precision.HIGHEST
F32, BF16 = jnp.float32, jnp.bfloat16

WIDTH = {"A+": 768, "A-": 768, "B+": 1280, "B-": 1280}
ROUTES = tuple(WIDTH)
START = {"A+": 0, "A-": 768, "B+": 1536, "B-": 2816}


def forwards(route, dx, dy):
    plus = route[1] == "+"
    up_x, down_x = ((0, 1), (0,)) if plus else ((0,), (0, 3))
    up_y, down_y = ((0, 1, 2, 3), (0, 7, 6)) if plus else ((0, 1, 2), (0, 7, 6, 5))
    out = []
    along_x = route[0] == "A" and dy == 0 or route[0] == "B"
    along_y = route[0] == "B" and dx == 0 or route[0] == "A"
    if along_y:
        if dy in up_y:
            out.append(("+y", dx, (dy + 1) % NY))
        if dy in down_y:
            out.append(("-y", dx, (dy - 1) % NY))
    if along_x:
        if dx in up_x:
            out.append(("+x", (dx + 1) % NX, dy))
        if dx in down_x:
            out.append(("-x", (dx - 1) % NX, dy))
    return out


def depth(route, dx, dy):
    return max((1 + depth(route, a, b) for _, a, b in forwards(route, dx, dy)), default=0)


def gather_plan():
    heap = [(0.0, i, r, 0, 0) for i, r in enumerate(("B+", "B-", "A+", "A-"))]
    free = dict.fromkeys(("+x", "-x", "+y", "-y"), 0.0)
    plan, count = [], 10
    while heap:
        when, _, route, dx, dy = heapq.heappop(heap)
        hops = sorted(forwards(route, dx, dy), key=lambda f: -depth(route, f[1], f[2]))
        plan.append((route, dx, dy, hops))
        for link, a, b in hops:
            free[link] = max(when, free[link]) + WIDTH[route] * 16 / 46.5e3 + 0.05
            count += 1
            heapq.heappush(heap, (free[link] + 1.6, count, route, a, b))
    return plan


def iota(shape, dim):
    return lax.broadcasted_iota(jnp.int32, shape, dim)


def kernel(
    img, refs, shifts, owners, slot_rows, interp, reg,
    vol, res,
    gat, rot, cos_t, sin_t, acc, wts, prod, part, own_tot, pair_s, pair_r, z_s, z_r,
    meta_s, meta_r, stat_s, stat_r, mz_s, mz_r, mb_s, mb_r, val_s, val_r, rep_s, rep_r,
    oh, oh_t, scat, scat_t, cnt,
    loc_sem, gat_send, gat_recv, pair_send, pair_recv, z_send, z_recv, sends, recvs,
):
    me_i, me_o = lax.axis_index("img"), lax.axis_index("ori")
    x, y = me_o // NY, lax.rem(me_o, NY)
    z, c = me_i // 2, lax.rem(me_i, 2)

    barrier = pltpu.get_barrier_semaphore()

    def greet_ori(p, carry):
        pl.semaphore_signal(barrier, 1, device_id={"ori": lax.rem(me_o + p, N_ORI)}, device_id_type=MESH)
        return carry

    def greet_img(p, carry):
        pl.semaphore_signal(barrier, 1, device_id={"img": lax.rem(me_i + p, N_IMG)}, device_id_type=MESH)
        return carry

    lax.fori_loop(1, N_ORI, greet_ori, 0)
    lax.fori_loop(1, N_IMG, greet_img, 0)

    own_copy = pltpu.make_async_copy(img, gat.at[me_o], loc_sem)
    own_copy.start()

    unit = 2.0 * math.pi / 128.0
    step_x, step_y = unit * shifts[:, 0:1], unit * shifts[:, 1:2]
    lane12 = iota((SHIFTS, 128), 1)
    base = step_x * (lane12 % 64).astype(F32) + step_y * (lane12 // 64).astype(F32)
    tile = step_y * (2 * lane12 - 64).astype(F32)
    base_c, base_s, tile_c, tile_s = jnp.cos(base), jnp.sin(base), jnp.cos(tile), jnp.sin(tile)
    for t in range(64):
        half, col = t // 32, (t % 32) * 128
        tc, ts = tile_c[:, t : t + 1], tile_s[:, t : t + 1]
        cos_t[half, :, col : col + 128] = base_c * tc - base_s * ts
        sin_t[half, :, col : col + 128] = base_s * tc + base_c * ts

    def rotate(step, carry):
        cols = pl.ds(pl.multiple_of(step * 256, 256), 256)
        for half in range(2):
            real = refs[:, pl.ds(pl.multiple_of(half * QUART + step * 256, 256), 256)].astype(F32)
            imag = refs[:, pl.ds(pl.multiple_of((2 + half) * QUART + step * 256, 256), 256)].astype(F32)
            for s in range(SHIFTS):
                cs, sn = cos_t[half, s : s + 1, cols], sin_t[half, s : s + 1, cols]
                rot[pl.ds(half * 192 + s * 16, 16), cols] = (real * cs - imag * sn).astype(BF16)
                rot[pl.ds((2 + half) * 192 + s * 16, 16), cols] = (real * sn + imag * cs).astype(BF16)
        return carry

    lax.fori_loop(0, QUART // 256, rotate, 0)

    eye = iota((128, 128), 0) == iota((128, 128), 1)
    row_col = jnp.sum(jnp.where(eye, slot_rows[...].astype(F32), 0.0), axis=1, keepdims=True)
    blocks = [(q * 32 + u * 8) for u in range(4) for q in range(4)]
    row_col = jnp.concatenate([row_col[b : b + 8] for b in blocks], axis=0)
    own_col = jnp.concatenate([owners[b : b + 8, :] for b in blocks], axis=0).astype(F32)
    lane128 = iota((128, 128), 1).astype(F32)
    owner_hot = (own_col == lane128).astype(F32)
    before = (iota((128, 128), 1) < iota((128, 128), 0)).astype(BF16)
    counts = jnp.dot(before, owner_hot.astype(BF16), preferred_element_type=F32)
    rank_col = jnp.sum(counts * owner_hot, axis=1, keepdims=True)
    slot_col = own_col * CAP + rank_col
    slot_row = jnp.sum(jnp.where(eye, slot_col, 0.0), axis=0, keepdims=True)
    oh[...] = (slot_row == iota((SLOTS, 128), 0).astype(F32)).astype(BF16)
    oh_t[...] = (slot_col == iota((128, SLOTS), 1).astype(F32)).astype(BF16)
    rank_rows = jnp.where(rank_col == lane128, row_col + 1.0, 0.0).astype(BF16)
    table = lax.dot_general(
        owner_hot.astype(BF16), rank_rows, (((0,), (0,)), ((), ())), preferred_element_type=F32
    ) - 1.0
    for d in range(N_ORI):
        meta_s[d] = table[d : d + 1, :]

    own_copy.wait()
    pl.semaphore_wait(barrier, N_ORI - 1 + N_IMG - 1)

    link = {
        "+x": lax.rem(x + 1, NX) * NY + y,
        "-x": lax.rem(x + NX - 1, NX) * NY + y,
        "+y": x * NY + lax.rem(y + 1, NY),
        "-y": x * NY + lax.rem(y + NY - 1, NY),
    }

    def gather_copy(route, dx, dy, to, there):
        src = lax.rem(x + NX - dx, NX) * NY + lax.rem(y + NY - dy, NY)
        ref = gat.at[src, :, pl.ds(START[route], WIDTH[route])]
        r = ROUTES.index(route)
        return pltpu.make_async_remote_copy(
            src_ref=ref, dst_ref=ref, send_sem=gat_send.at[r], recv_sem=gat_recv.at[r, there],
            device_id={"ori": to}, device_id_type=MESH,
        )

    def spread(send_ref, recv_ref, number):
        def one(p, carry):
            to = lax.rem(me_o + p, N_ORI)
            src = send_ref.at[0] if send_ref.shape[0] == 1 else send_ref.at[to]
            pltpu.make_async_remote_copy(
                src_ref=src, dst_ref=recv_ref.at[me_o], send_sem=sends.at[number], recv_sem=recvs.at[number],
                device_id={"ori": to}, device_id_type=MESH,
            ).start()
            return carry

        lax.fori_loop(1, N_ORI, one, 0)

    def await_bytes(ref, sem):
        pltpu.make_async_copy(ref, ref, sem).wait()

    for route, dx, dy, hops in gather_plan():
        if dx or dy:
            gather_copy(route, dx, dy, me_o, dx * NY + dy).wait_recv()
        for name, a, b in hops:
            gather_copy(route, dx, dy, link[name], a * NY + b).start()
        if (route, dx, dy) == ("A-", 0, 0):
            spread(meta_s, meta_r, 0)
            meta_r[me_o] = meta_s[me_o]

    acc[...] = jnp.zeros_like(acc)

    def score(step, carry):
        cols = pl.ds(pl.multiple_of(step * 512, 512), 512)
        block = gat[:, :, cols].reshape(N_ORI * 8, 512)
        acc[...] += lax.dot_general(rot[:, cols], block, (((1,), (1,)), ((), ())), preferred_element_type=F32)
        return carry

    lax.fori_loop(0, QUART // 512, score, 0)

    lane = iota((192, 256), 1)
    mine = jnp.zeros((192, 256), F32)
    for q in range(4):
        mine = mine + jnp.where(lane % 4 == q, acc[q * 192 : (q + 1) * 192, :], 0.0)
    fold = (iota((256, 256), 0) // 4 == iota((256, 256), 1) // 4).astype(F32)
    scores = jnp.dot(mine, fold, precision=HIGH, preferred_element_type=F32) * (2.0 / math.sqrt(COEF))
    peak = jnp.max(scores, axis=0, keepdims=True)
    expo = jnp.exp(scores - peak)
    total = jnp.sum(expo, axis=0, keepdims=True)
    stat = jnp.where(iota((1, 256), 1) % 2 == 0, peak, total)
    stat_s[0] = stat
    spread(stat_s, stat_r, 1)
    stat_r[me_o] = stat

    await_bytes(meta_r.at[pl.ds(0, N_ORI - 1)], recvs.at[0])
    rep = (iota((SLOTS, N_ORI), 0) // CAP == iota((SLOTS, N_ORI), 1)).astype(BF16)
    rid = jnp.dot(rep, meta_r[...].reshape(N_ORI, 128).astype(BF16), preferred_element_type=F32)
    rid = jnp.where(iota((SLOTS, 128), 0) % CAP == iota((SLOTS, 128), 1), rid, 0.0)
    hot = (jnp.sum(rid, axis=1, keepdims=True) == iota((SLOTS, 128), 1).astype(F32)).astype(F32)
    scat_t[...] = hot.astype(BF16)
    scat[...] = jnp.transpose(hot).astype(BF16)
    cnt[...] = jnp.dot(scat[...], rep, preferred_element_type=F32)
    reg_col = jnp.sum(
        jnp.where(iota((ROWS, ROWS), 0) == iota((ROWS, ROWS), 1), reg[...], 0.0), axis=1, keepdims=True
    )

    await_bytes(stat_r.at[pl.ds(0, N_ORI - 1)], recvs.at[1])
    stats = stat_r[...].reshape(N_ORI, 256)
    even = iota((N_ORI, 256), 1) % 2 == 0
    peaks = jnp.where(even, stats, pltpu.roll(stats, 1, 1))
    totals = jnp.where(even, pltpu.roll(stats, 255, 1), stats)
    top = jnp.max(peaks, axis=0, keepdims=True)
    whole = jnp.sum(totals * jnp.exp(peaks - top), axis=0, keepdims=True)
    weights = expo * (jnp.exp(peak - top) / whole)
    for q in range(4):
        wts[q * 192 : (q + 1) * 192, :] = jnp.where(lane % 4 == q, weights, 0.0).astype(BF16)

    mass = jnp.sum(jnp.where(lane % 4 == 0, weights, 0.0), axis=1, keepdims=True)
    mass16 = mass[0:16]
    for s in range(1, SHIFTS):
        mass16 = mass16 + mass[s * 16 : s * 16 + 16]
    mass16 = jnp.broadcast_to(mass16, (16, 128))
    for o in range(N_IMG):
        mz_s[o] = mass16[o : o + 1, :]

    def send_mass(p, carry):
        to = lax.rem(me_i + p, N_IMG)
        pltpu.make_async_remote_copy(
            src_ref=mz_s.at[to], dst_ref=mz_r.at[me_i], send_sem=sends.at[2], recv_sem=recvs.at[2],
            device_id={"img": to}, device_id_type=MESH,
        ).start()
        return carry

    lax.fori_loop(1, N_IMG, send_mass, 0)
    mz_r[me_i] = mz_s[me_i]

    def pair_copy(u):
        return pltpu.make_async_remote_copy(
            src_ref=pair_s.at[u], dst_ref=pair_r.at[u], send_sem=pair_send.at[u], recv_sem=pair_recv.at[u],
            device_id={"img": z * 2 + 1 - c}, device_id_type=MESH,
        )

    def project(u, carry):
        for v in range(4):
            cols = pl.ds(pl.multiple_of(u * 1024 + v * 256, 256), 256)
            block = gat[:, :, cols].reshape(N_ORI * 8, 256)
            prod[...] = jnp.dot(wts[...], block, preferred_element_type=F32)
            for half in range(2):
                re = jnp.zeros((16, 256), F32)
                im = jnp.zeros((16, 256), F32)
                for s in range(SHIFTS):
                    cs, sn = cos_t[half, s : s + 1, cols], sin_t[half, s : s + 1, cols]
                    sr = prod[half * 192 + s * 16 : half * 192 + s * 16 + 16, :]
                    si = prod[(2 + half) * 192 + s * 16 : (2 + half) * 192 + s * 16 + 16, :]
                    re = re + sr * cs + si * sn
                    im = im - sr * sn + si * cs
                for a in range(2):
                    part[u, :, half * 8 + v * 2 + a, :] = re[:, a * 128 : a * 128 + 128]
                    part[u, :, (2 + half) * 8 + v * 2 + a, :] = im[:, a * 128 : a * 128 + 128]
        for k in range(NZ):
            pair_s[u, k] = part[u, 2 * k + 1 - c].astype(BF16)
        pair_copy(u).start()
        return carry

    def reduce_pair(u):
        pair_copy(u).wait_recv()
        own_tot[u] = part[u, 2 * z + c] + pair_r[u, z].astype(F32)
        for p in (4, 3, 5, 2, 6, 1, 7):
            to = lax.rem(z + p, NZ)
            z_s[u, to] = (part[u, 2 * to + c] + pair_r[u, to].astype(F32)).astype(BF16)
            pltpu.make_async_remote_copy(
                src_ref=z_s.at[u, to], dst_ref=z_r.at[u, z], send_sem=z_send.at[u], recv_sem=z_recv.at[u],
                device_id={"img": to * 2 + c}, device_id_type=MESH,
            ).start()

    def project_and_reduce(u, carry):
        project(u, 0)
        reduce_pair(u - 1)
        return carry

    project(0, 0)
    lax.fori_loop(1, 4, project_and_reduce, 0)
    reduce_pair(3)

    await_bytes(mz_r.at[pl.ds(0, N_IMG - 1)], recvs.at[2])
    mass_all = jnp.sum(mz_r[...].reshape(N_IMG, 128), axis=0, keepdims=True)
    mb_s[0] = mass_all
    spread(mb_s, mb_r, 3)
    mb_r[me_o] = mass_all

    sums = []
    for u in range(4):
        await_bytes(z_r.at[u, pl.ds(0, NZ - 1)], z_recv.at[u])
        tot = own_tot[u]
        for p in range(1, NZ):
            tot = tot + z_r[u, lax.rem(z + p, NZ)].astype(F32)
        sums.append(tot)
    segments = jnp.concatenate(sums, axis=0).astype(BF16)

    val_s[...] = jnp.dot(oh[...], segments, preferred_element_type=F32).astype(BF16).reshape(N_ORI, CAP, 128)
    spread(val_s, val_r, 4)
    val_r[me_o] = val_s[me_o]

    await_bytes(mb_r.at[pl.ds(0, N_ORI - 1)], recvs.at[3])
    weight_sum = jnp.dot(
        cnt[0:ROWS, :], mb_r[...].reshape(N_ORI, 128), precision=HIGH, preferred_element_type=F32
    )
    denom = weight_sum + reg_col

    await_bytes(val_r.at[pl.ds(0, N_ORI - 1)], recvs.at[4])
    inserted = jnp.dot(scat[0:ROWS, :], val_r[...].reshape(SLOTS, 128), preferred_element_type=F32)
    mapped = jnp.dot(inserted, interp[...], precision=HIGH, preferred_element_type=F32)
    volume = mapped / denom
    vol[...] = volume
    back = lax.dot_general(
        volume, interp[...], (((1,), (1,)), ((), ())), precision=HIGH, preferred_element_type=F32
    )
    reply = jnp.dot(scat_t[:, 0:ROWS], back.astype(BF16), preferred_element_type=F32)
    rep_s[...] = reply.astype(BF16).reshape(N_ORI, CAP, 128)
    spread(rep_s, rep_r, 5)
    rep_r[me_o] = rep_s[me_o]

    for r, route in enumerate(ROUTES):
        await_bytes(gat.at[pl.ds(0, N_ORI - 1), :, pl.ds(START[route], WIDTH[route])], gat_send.at[r])
    for u in range(4):
        pair_copy(u).wait_send()
        await_bytes(z_s.at[u, pl.ds(0, NZ - 1)], z_send.at[u])
    await_bytes(meta_s.at[pl.ds(0, N_ORI - 1)], sends.at[0])
    await_bytes(stat_r.at[pl.ds(0, N_ORI - 1)], sends.at[1])
    await_bytes(mz_s.at[pl.ds(0, N_IMG - 1)], sends.at[2])
    await_bytes(mb_r.at[pl.ds(0, N_ORI - 1)], sends.at[3])
    await_bytes(val_s.at[pl.ds(0, N_ORI - 1)], sends.at[4])

    await_bytes(rep_r.at[pl.ds(0, N_ORI - 1)], recvs.at[5])
    picked = jnp.dot(oh_t[...], rep_r[...].reshape(SLOTS, 128), preferred_element_type=F32)
    for u in range(4):
        for q in range(4):
            res[q * 32 + u * 8 : q * 32 + u * 8 + 8, :] = picked[u * 32 + q * 8 : u * 32 + q * 8 + 8, :]
    await_bytes(rep_s.at[pl.ds(0, N_ORI - 1)], sends.at[5])


def shards(images, references, shifts, owners, slot_rows, interpolation, regularizer):
    vmem = pl.BlockSpec(memory_space=pltpu.VMEM)
    volume, resampled = pl.pallas_call(
        kernel,
        out_shape=(jax.ShapeDtypeStruct((ROWS, 128), F32), jax.ShapeDtypeStruct((128, 128), F32)),
        in_specs=[vmem] * 7,
        out_specs=(vmem, vmem),
        scratch_shapes=[
            pltpu.VMEM((N_ORI, 8, QUART), BF16),
            pltpu.VMEM((768, QUART), BF16),
            pltpu.VMEM((2, SHIFTS, QUART), F32),
            pltpu.VMEM((2, SHIFTS, QUART), F32),
            pltpu.VMEM((768, 256), F32),
            pltpu.VMEM((768, 256), BF16),
            pltpu.VMEM((768, 256), F32),
            pltpu.VMEM((4, N_IMG, 32, 128), F32),
            pltpu.VMEM((4, 32, 128), F32),
            pltpu.VMEM((4, NZ, 32, 128), BF16),
            pltpu.VMEM((4, NZ, 32, 128), BF16),
            pltpu.VMEM((4, NZ, 32, 128), BF16),
            pltpu.VMEM((4, NZ, 32, 128), BF16),
            pltpu.VMEM((N_ORI, 1, 128), F32),
            pltpu.VMEM((N_ORI, 1, 128), F32),
            pltpu.VMEM((1, 1, 256), F32),
            pltpu.VMEM((N_ORI, 1, 256), F32),
            pltpu.VMEM((N_IMG, 1, 128), F32),
            pltpu.VMEM((N_IMG, 1, 128), F32),
            pltpu.VMEM((1, 1, 128), F32),
            pltpu.VMEM((N_ORI, 1, 128), F32),
            pltpu.VMEM((N_ORI, CAP, 128), BF16),
            pltpu.VMEM((N_ORI, CAP, 128), BF16),
            pltpu.VMEM((N_ORI, CAP, 128), BF16),
            pltpu.VMEM((N_ORI, CAP, 128), BF16),
            pltpu.VMEM((SLOTS, 128), BF16),
            pltpu.VMEM((128, SLOTS), BF16),
            pltpu.VMEM((128, SLOTS), BF16),
            pltpu.VMEM((SLOTS, 128), BF16),
            pltpu.VMEM((128, N_ORI), F32),
            pltpu.SemaphoreType.DMA,
            pltpu.SemaphoreType.DMA((4,)),
            pltpu.SemaphoreType.DMA((4, N_ORI)),
            pltpu.SemaphoreType.DMA((4,)),
            pltpu.SemaphoreType.DMA((4,)),
            pltpu.SemaphoreType.DMA((4,)),
            pltpu.SemaphoreType.DMA((4,)),
            pltpu.SemaphoreType.DMA((6,)),
            pltpu.SemaphoreType.DMA((6,)),
        ],
        compiler_params=pltpu.CompilerParams(
            collective_id=0, has_side_effects=True, vmem_limit_bytes=48 * 1024 * 1024
        ),
    )(
        images.reshape(8, QUART),
        references,
        shifts,
        owners,
        slot_rows.reshape(1, 128),
        interpolation,
        regularizer.reshape(1, ROWS),
    )
    return (volume, resampled.reshape(1, COEF))


def solution(mesh):
    in_specs = (
        P(("img", "ori"), None),
        P("ori", None),
        P(),
        P(("ori", "img"), None),
        P(("ori", "img")),
        P(("ori", "img"), None),
        P(("ori", "img")),
    )
    out_specs = (P(("ori", "img"), None), P(("ori", "img"), None))
    return jax.shard_map(shards, mesh=mesh, in_specs=in_specs, out_specs=out_specs, check_vma=False)
```

time: 434 us -> 79.8 us (0.18)
  the two profiles are of different devices: /device:TPU:8 before, /device:TPU:16 now
where the time goes in v1:
time: 79.8 us; the launch traced here: 79.5 us
  Pallas kernels  74.1 us (93%)
  local copies, waits for them, and re-layouts  4.77 us (6%)
    pallas_call x1, Pallas kernels, shards(): pl.pallas_call(kernel, out_shape=(jax.ShapeDtypeStruct((ROWS, 128), F32),...  74.1 us
    unnamed x16, local copies, waits for them, and re-layouts  3.89 us

profile of v1, /device:TPU:16, one launch (start us, length us, event | category | flops | bytes accessed | tf_op | source)
XLA Modules:
  0.0 79.5 jit_solution(10534550390883918228)
XLA Ops:
  0.6 0.0 copy-start.4
  0.6 0.7 copy-done.4
  1.3 0.1 copy.9.shifts
  1.4 0.0 copy-start.5
  1.4 0.0 copy-start.3
  1.4 0.9 %reshape.16.img = bf16[8,4096]{1,0:T(8,128)(2,1)S(1)} reshape(bf16[2,16384]{1,0:T(2,128)(2,1)} %param.7) | data formatting | bytes 131072 | tf_op jit(solution)/shard_map/reshape | solution.py:412
  2.3 0.0 copy-done.5
  2.3 0.0 copy-start.1
  2.3 0.0 copy-start.2
  2.3 0.1 copy.10.owners
  2.4 0.0 copy-done.3
  2.4 0.7 copy-done.1
  3.2 0.0 copy-done.2
  3.2 0.0 copy-start
  3.2 1.0 %copy-done = bf16[16,16384]{1,0:T(8,128)(2,1)S(1)} copy-done((bf16[16,16384]{1,0:T(8,128)(2,1)S(1)}, bf16[16,16384]{1,0:T(8,128)(2,1)}, u32[]{:S(2)}) %copy-start) | copy-done | bytes 524312
  4.2 74.1 %shard_map.86 = (f32[64,128]{1,0:T(8,128)S(1)}, f32[128,128]{1,0:T(8,128)S(1)}) custom-call(bf16[8,4096]{1,0:T(8,128)(2,1)S(1)} %reshape.16.img, bf16[16,16384]{1,0:T(8,128)(2,1)S(1)} %copy-done, f32[12,2]{1,0:T(8,128)S(1)} %copy.9.shifts, s32[128,1]{1,0:T(8,128)S(1)} %copy.10.owners, s32[1,128]{1,0:T(1,128)S(1)} %bitcast.4, f32[128,128]{1,0:T(8,128)S(1)} %copy-done.1, ...), custom_call_target="tpu_custom_call" | custom-call | tf_op jit(solution)/shard_map/pallas_call | solution.py:362
  78.3 0.6 copy.13
  78.9 0.6 copy.14
Async XLA Ops:
  0.6 0.7 copy-start.4
  1.4 0.9 %copy-start.5 = (s32[128,1]{0,1:T(1,128)S(1)}, s32[128,1]{0,1:T(1,128)}, u32[]{:S(2)}) copy-start(s32[128,1]{0,1:T(1,128)} %param.10) | copy-start | bytes 1540
  1.4 1.0 %copy-start.3 = (f32[64]{0:T(128)S(1)}, f32[64]{0:T(128)}, u32[]{:S(2)}) copy-start(f32[64]{0:T(128)} %param.13) | copy-start | bytes 772
  2.3 0.8 %copy-start.1 = (f32[128,128]{1,0:T(8,128)S(1)}, f32[128,128]{1,0:T(8,128)}, u32[]{:S(2)}) copy-start(f32[128,128]{1,0:T(8,128)} %interp.1) | copy-start | bytes 196612
  2.3 0.8 %copy-start.2 = (s32[128]{0:T(128)S(1)}, s32[128]{0:T(128)}, u32[]{:S(2)}) copy-start(s32[128]{0:T(128)} %param.11) | copy-start | bytes 1540
  3.2 1.0 %copy-start = (bf16[16,16384]{1,0:T(8,128)(2,1)S(1)}, bf16[16,16384]{1,0:T(8,128)(2,1)}, u32[]{:S(2)}) copy-start(bf16[16,16384]{1,0:T(8,128)(2,1)} %refs.1) | copy-start | bytes 1572868

commit v2 on v1

v2 whole, which is shorter than its diff:
```python
import heapq
import math

import jax
import jax.numpy as jnp
from jax import lax
from jax.experimental import pallas as pl
from jax.experimental.pallas import tpu as pltpu
from jax.sharding import PartitionSpec as P

NX, NY, NZ = 4, 8, 8
N_ORI = NX * NY
N_IMG = 2 * NZ
COEF = 16384
QUART = COEF // 4
SHIFTS = 12
CAP = 16
SLOTS = N_ORI * CAP
ROWS = 64
MESH = pl.DeviceIdType.MESH
SCORE_COLS = 2048
HIGH = lax.Precision.HIGHEST
F32, BF16 = jnp.float32, jnp.bfloat16

SPLIT = 1536
RANGE = {"A": (0, SPLIT), "B": (SPLIT, QUART)}
PARENT = {"A": ((0, 0, 1), (0, 0, 1, 2, 2)), "B": ((0, 0, 1), (0, 0, 0, 2, 2))}


def ring_steps(parents, size, d, sign, lo, hi, mid):
    for k in range(1, size // 2 + 1):
        for way in (1, -1):
            if d != way * parents[k] % size or d and sign != way:
                continue
            a, b = lo, hi
            if k == size // 2:
                a, b = (lo, min(hi, mid)) if way > 0 else (max(lo, mid), hi)
            if a < b:
                yield way, way * k % size, k - parents[k], a, b


def forwards(block):
    route, lo, hi, dx, dy, sx, sy = block
    mid = sum(RANGE[route]) // 2
    par_x, par_y = PARENT[route]
    out = []
    if route == "A" or dx == 0:
        for way, d, hops, a, b in ring_steps(par_y, NY, dy, sy, lo, hi, mid):
            out.append(("y", way * hops, (route, a, b, dx, d, sx, way)))
    if route == "B" or dy == 0:
        for way, d, hops, a, b in ring_steps(par_x, NX, dx, sx, lo, hi, mid):
            out.append(("x", way * hops, (route, a, b, d, dy, way, sy)))
    return out


def depth(block):
    return max((1.4 + 0.7 * abs(h) + depth(k) for _, h, k in forwards(block)), default=0)


def gather_plan():
    heap = [(0.0, i, (r, *RANGE[r], 0, 0, 0, 0)) for i, r in enumerate("BA")]
    free, plan, count = {}, [], 10
    while heap:
        when, _, block = heapq.heappop(heap)
        hops = sorted(forwards(block), key=lambda f: -depth(f[2]) - 0.7 * abs(f[1]))
        plan.append((block, hops))
        for axis, dist, to in hops:
            wire = axis, dist > 0
            took = (to[2] - to[1]) * 16 / 46.5e3 + 0.03
            begin = max(when, free.get(wire, 0.0))
            free[wire] = begin + took * abs(dist)
            count += 1
            heapq.heappush(heap, (begin + took + 1.4 + 0.7 * abs(dist), count, to))
    return plan


def iota(shape, dim):
    return lax.broadcasted_iota(jnp.int32, shape, dim)


def kernel(
    images_h, refs_h, shifts_h, owners_h, rows_h, interp_h, reg_h,
    vol, res,
    images, refs, shifts, owners, slot_rows, interp, reg,
    gat, rot, cos_t, sin_t, acc, wts, part, own_tot, pair_s, pair_r, z_s, z_r,
    meta_s, meta_r, stat_s, stat_r, mz_s, mz_r, mb_s, mb_r, val_s, val_r, rep_s, rep_r,
    oh, oh_t, scat, scat_t, cnt,
    loc_sem, gat_send, gat_recv, pair_send, pair_recv, z_send, z_recv, sends, recvs, token,
):
    me_i, me_o = lax.axis_index("img"), lax.axis_index("ori")
    x, y = me_o // NY, lax.rem(me_o, NY)
    z, c = me_i // 2, lax.rem(me_i, 2)
    up, down = lax.rem(z + 1, NZ) * 2 + c, lax.rem(z + NZ - 1, NZ) * 2 + c

    def along(axis, dist):
        if axis == "x":
            return lax.rem(x + NX + dist, NX) * NY + y
        return x * NY + lax.rem(y + NY + dist, NY)

    plan = gather_plan()
    number = {block: i for i, (block, _) in enumerate(plan)}
    near = sorted({(axis, dist) for _, hops in plan for axis, dist, _ in hops})
    barrier = pltpu.get_barrier_semaphore()
    for axis, dist in near:
        pl.semaphore_signal(barrier, 1, device_id={"ori": along(axis, dist)}, device_id_type=MESH)
    for to in (up, down, z * 2 + 1 - c):
        pl.semaphore_signal(barrier, 1, device_id={"img": to}, device_id_type=MESH)

    loads = [
        pltpu.make_async_copy(src, dst, loc_sem.at[i])
        for i, (src, dst) in enumerate(
            [(images_h, images), (shifts_h, shifts), (refs_h, refs), (owners_h, owners), (rows_h, slot_rows),
             (interp_h, interp), (reg_h, reg)]
        )
    ]
    for copy in loads:
        copy.start()

    loads[0].wait()
    gat[me_o] = jnp.concatenate(
        [images[:, q * QUART : (q + 1) * QUART].astype(F32) for q in range(4)], axis=0
    ).astype(BF16)
    loads[1].wait()

    unit = 2.0 * math.pi / 128.0
    eye12 = iota((SHIFTS, SHIFTS), 0) == iota((SHIFTS, SHIFTS), 1)
    step_x = unit * jnp.sum(jnp.where(eye12, shifts[0:1, :], 0.0), axis=1, keepdims=True)
    step_y = unit * jnp.sum(jnp.where(eye12, shifts[1:2, :], 0.0), axis=1, keepdims=True)

    def tables(step):
        lane12 = iota((SHIFTS, 128), 1)
        base = step_x * (lane12 % 64).astype(F32) + step_y * (lane12 // 64).astype(F32)
        tile = step_y * (2 * lane12 - 64).astype(F32)
        base_c, base_s, tile_c, tile_s = jnp.cos(base), jnp.sin(base), jnp.cos(tile), jnp.sin(tile)
        for t in range(64):
            half, col = t // 32, (t % 32) * 128
            tc, ts = tile_c[:, t : t + 1], tile_s[:, t : t + 1]
            cos_t[half, :, col : col + 128] = base_c * tc - base_s * ts
            sin_t[half, :, col : col + 128] = base_s * tc + base_c * ts

    def rotate(step):
        if step == 0:
            loads[2].wait()
        col = step * 256
        for half in range(2):
            real = refs[:, half * QUART + col : half * QUART + col + 256].astype(F32)
            imag = refs[:, (2 + half) * QUART + col : (2 + half) * QUART + col + 256].astype(F32)
            for s in range(SHIFTS):
                cs, sn = cos_t[half, s : s + 1, col : col + 256], sin_t[half, s : s + 1, col : col + 256]
                rot[half * 192 + s * 16 : half * 192 + s * 16 + 16, col : col + 256] = (
                    real * cs - imag * sn
                ).astype(BF16)
                rot[(2 + half) * 192 + s * 16 : (2 + half) * 192 + s * 16 + 16, col : col + 256] = (
                    real * sn + imag * cs
                ).astype(BF16)

    def routing(step):
        loads[3].wait()
        loads[4].wait()
        eye = iota((128, 128), 0) == iota((128, 128), 1)
        row_col = jnp.sum(jnp.where(eye, slot_rows[...].astype(F32), 0.0), axis=1, keepdims=True)
        own_col = jnp.sum(jnp.where(eye, owners[...].astype(F32), 0.0), axis=1, keepdims=True)
        blocks = [(q * 32 + u * 8) for u in range(4) for q in range(4)]
        row_col = jnp.concatenate([row_col[b : b + 8] for b in blocks], axis=0)
        own_col = jnp.concatenate([own_col[b : b + 8] for b in blocks], axis=0)
        lane128 = iota((128, 128), 1).astype(F32)
        owner_hot = (own_col == lane128).astype(F32)
        before = (iota((128, 128), 1) < iota((128, 128), 0)).astype(BF16)
        counts = jnp.dot(before, owner_hot.astype(BF16), preferred_element_type=F32)
        rank_col = jnp.sum(counts * owner_hot, axis=1, keepdims=True)
        slot_col = own_col * CAP + rank_col
        slot_row = jnp.sum(jnp.where(eye, slot_col, 0.0), axis=0, keepdims=True)
        oh[...] = (slot_row == iota((SLOTS, 128), 0).astype(F32)).astype(BF16)
        oh_t[...] = (slot_col == iota((128, SLOTS), 1).astype(F32)).astype(BF16)
        rank_rows = jnp.where(rank_col == lane128, row_col + 1.0, 0.0).astype(BF16)
        table = lax.dot_general(
            owner_hot.astype(BF16), rank_rows, (((0,), (0,)), ((), ())), preferred_element_type=F32
        ) - 1.0
        for d in range(N_ORI):
            meta_s[d] = table[d : d + 1, :]

    def pass_token(step):
        if step:
            for way in range(2):
                pl.semaphore_wait(token.at[step - 1, way], 1)
        if step < 4:
            for way, to in enumerate((up, down)):
                pl.semaphore_signal(token.at[step, way], 1, device_id={"img": to}, device_id_type=MESH)

    pl.semaphore_wait(barrier, len(near) + 3)

    def gather_copy(block, dx, dy, to):
        src = lax.rem(x + NX - dx, NX) * NY + lax.rem(y + NY - dy, NY)
        ref = gat.at[src, :, pl.ds(block[1], block[2] - block[1])]
        return pltpu.make_async_remote_copy(
            src_ref=ref, dst_ref=ref, send_sem=gat_send, recv_sem=gat_recv.at[number[block]],
            device_id={"ori": to}, device_id_type=MESH,
        )

    def spread(send_ref, recv_ref, which):
        def one(p, carry):
            to = lax.rem(me_o + p, N_ORI)
            src = send_ref.at[0] if send_ref.shape[0] == 1 else send_ref.at[to]
            pltpu.make_async_remote_copy(
                src_ref=src, dst_ref=recv_ref.at[me_o], send_sem=sends.at[which], recv_sem=recvs.at[which],
                device_id={"ori": to}, device_id_type=MESH,
            ).start()
            return carry

        lax.fori_loop(1, N_ORI, one, 0)

    def await_bytes(ref, sem):
        pltpu.make_async_copy(ref, ref, sem).wait()

    jobs = [(pass_token, 0), (tables, 0)]
    jobs += [(rotate, i) for i in range(QUART // 256)]
    jobs[6:6] = [(pass_token, 1)]
    jobs[10:10] = [(pass_token, 2)]
    jobs[14:14] = [(pass_token, 3)]
    jobs += [(pass_token, 4), (routing, 0)]
    due = [2 + i * (len(plan) - 8) // len(jobs) for i in range(len(jobs))]
    for i, (block, hops) in enumerate(plan):
        dx, dy = block[3:5]
        if dx or dy:
            gather_copy(block, dx, dy, me_o).wait_recv()
        for axis, dist, to in hops:
            gather_copy(to, dx, dy, along(axis, dist)).start()
        while due and due[0] <= i:
            due.pop(0)
            job, step = jobs.pop(0)
            job(step)
    for job, step in jobs:
        job(step)
    spread(meta_s, meta_r, 0)
    meta_r[me_o] = meta_s[me_o]

    def score(step, carry):
        cols = pl.ds(step * SCORE_COLS if isinstance(step, int) else pl.multiple_of(step * SCORE_COLS, SCORE_COLS), SCORE_COLS)
        block = gat[:, :, cols].reshape(N_ORI * 8, SCORE_COLS)
        got = lax.dot_general(rot[:, cols], block, (((1,), (1,)), ((), ())), preferred_element_type=F32)
        acc[...] = got if isinstance(step, int) else acc[...] + got
        return carry

    score(0, 0)
    if QUART > SCORE_COLS:
        lax.fori_loop(1, QUART // SCORE_COLS, score, 0)

    lane = iota((192, 256), 1)
    quarter = lane % 8 // 2
    mine = jnp.zeros((192, 256), F32)
    for q in range(4):
        mine = mine + jnp.where(quarter == q, acc[q * 192 : (q + 1) * 192, :], 0.0)
    left, right = iota((256, 256), 0), iota((256, 256), 1)
    fold = ((left // 8 == right // 8) & (left % 2 == right % 2)).astype(F32)
    scores = jnp.dot(mine, fold, precision=HIGH, preferred_element_type=F32) * (2.0 / math.sqrt(COEF))
    peak = jnp.max(scores, axis=0, keepdims=True)
    expo = jnp.exp(scores - peak)
    total = jnp.sum(expo, axis=0, keepdims=True)
    stat = jnp.where(iota((1, 256), 1) // 2 % 2 == 0, peak, total)
    stat_s[0] = stat
    spread(stat_s, stat_r, 1)
    stat_r[me_o] = stat

    await_bytes(meta_r.at[pl.ds(0, N_ORI - 1)], recvs.at[0])
    rep = (iota((SLOTS, N_ORI), 0) // CAP == iota((SLOTS, N_ORI), 1)).astype(BF16)
    rid = jnp.dot(rep, meta_r[...].reshape(N_ORI, 128).astype(BF16), preferred_element_type=F32)
    rid = jnp.where(iota((SLOTS, 128), 0) % CAP == iota((SLOTS, 128), 1), rid, 0.0)
    hot = (jnp.sum(rid, axis=1, keepdims=True) == iota((SLOTS, 128), 1).astype(F32)).astype(F32)
    scat_t[...] = hot.astype(BF16)
    scat[...] = jnp.transpose(hot).astype(BF16)
    cnt[...] = jnp.dot(scat[...], rep, preferred_element_type=F32)
    loads[6].wait()
    reg_col = jnp.sum(
        jnp.where(iota((ROWS, ROWS), 0) == iota((ROWS, ROWS), 1), reg[...], 0.0), axis=1, keepdims=True
    )

    loads[5].wait()
    await_bytes(stat_r.at[pl.ds(0, N_ORI - 1)], recvs.at[1])
    stats = stat_r[...].reshape(N_ORI, 256)
    even = iota((N_ORI, 256), 1) // 2 % 2 == 0
    peaks = jnp.where(even, stats, pltpu.roll(stats, 2, 1))
    totals = jnp.where(even, pltpu.roll(stats, 254, 1), stats)
    top = jnp.max(peaks, axis=0, keepdims=True)
    whole = jnp.sum(totals * jnp.exp(peaks - top), axis=0, keepdims=True)
    weights = expo * (jnp.exp(peak - top) / whole)
    for q in range(4):
        wts[q * 192 : (q + 1) * 192, :] = jnp.where(quarter == q, weights, 0.0).astype(BF16)

    mass = jnp.sum(jnp.where(quarter == 0, weights, 0.0), axis=1, keepdims=True)
    mass16 = mass[0:16]
    for s in range(1, SHIFTS):
        mass16 = mass16 + mass[s * 16 : s * 16 + 16]
    mass16 = jnp.broadcast_to(mass16, (16, 128))
    for o in range(N_IMG):
        mz_s[o] = mass16[o : o + 1, :]

    def send_mass(p, carry):
        to = lax.rem(me_i + p, N_IMG)
        pltpu.make_async_remote_copy(
            src_ref=mz_s.at[to], dst_ref=mz_r.at[me_i], send_sem=sends.at[2], recv_sem=recvs.at[2],
            device_id={"img": to}, device_id_type=MESH,
        ).start()
        return carry

    lax.fori_loop(1, N_IMG, send_mass, 0)
    mz_r[me_i] = mz_s[me_i]

    def pair_copy(u):
        return pltpu.make_async_remote_copy(
            src_ref=pair_s.at[u], dst_ref=pair_r.at[u], send_sem=pair_send.at[u], recv_sem=pair_recv.at[u],
            device_id={"img": z * 2 + 1 - c}, device_id_type=MESH,
        )

    def project(u, carry):
        for v in range(4):
            cols = pl.ds(pl.multiple_of(u * 1024 + v * 256, 256), 256)
            block = gat[:, :, cols].reshape(N_ORI * 8, 256)
            prod = jnp.dot(wts[...], block, preferred_element_type=F32)
            for half in range(2):
                re = jnp.zeros((16, 256), F32)
                im = jnp.zeros((16, 256), F32)
                for s in range(SHIFTS):
                    cs, sn = cos_t[half, s : s + 1, cols], sin_t[half, s : s + 1, cols]
                    sr = prod[half * 192 + s * 16 : half * 192 + s * 16 + 16, :]
                    si = prod[(2 + half) * 192 + s * 16 : (2 + half) * 192 + s * 16 + 16, :]
                    re = re + sr * cs + si * sn
                    im = im - sr * sn + si * cs
                for a in range(2):
                    part[u, :, half * 8 + v * 2 + a, :] = re[:, a * 128 : a * 128 + 128]
                    part[u, :, (2 + half) * 8 + v * 2 + a, :] = im[:, a * 128 : a * 128 + 128]
        for k in range(NZ):
            pair_s[u, k] = part[u, 2 * k + 1 - c].astype(BF16)
        pair_copy(u).start()
        return carry

    def reduce_pair(u):
        pair_copy(u).wait_recv()
        own_tot[u] = part[u, 2 * z + c] + pair_r[u, z].astype(F32)
        for p in (4, 3, 5, 2, 6, 1, 7):
            to = lax.rem(z + p, NZ)
            z_s[u, to] = (part[u, 2 * to + c] + pair_r[u, to].astype(F32)).astype(BF16)
            pltpu.make_async_remote_copy(
                src_ref=z_s.at[u, to], dst_ref=z_r.at[u, z], send_sem=z_send.at[u], recv_sem=z_recv.at[u],
                device_id={"img": to * 2 + c}, device_id_type=MESH,
            ).start()

    def project_and_reduce(u, carry):
        project(u, 0)
        reduce_pair(u - 1)
        return carry

    project(0, 0)
    lax.fori_loop(1, 4, project_and_reduce, 0)
    reduce_pair(3)

    await_bytes(mz_r.at[pl.ds(0, N_IMG - 1)], recvs.at[2])
    mass_all = jnp.sum(mz_r[...].reshape(N_IMG, 128), axis=0, keepdims=True)
    mb_s[0] = mass_all
    spread(mb_s, mb_r, 3)
    mb_r[me_o] = mass_all

    sums = []
    for u in range(4):
        await_bytes(z_r.at[u, pl.ds(0, NZ - 1)], z_recv.at[u])
        tot = own_tot[u]
        for p in range(1, NZ):
            tot = tot + z_r[u, lax.rem(z + p, NZ)].astype(F32)
        sums.append(tot)
    segments = jnp.concatenate(sums, axis=0).astype(BF16)

    val_s[...] = jnp.dot(oh[...], segments, preferred_element_type=F32).astype(BF16).reshape(N_ORI, CAP, 128)
    spread(val_s, val_r, 4)
    val_r[me_o] = val_s[me_o]

    await_bytes(mb_r.at[pl.ds(0, N_ORI - 1)], recvs.at[3])
    weight_sum = jnp.dot(
        cnt[0:ROWS, :], mb_r[...].reshape(N_ORI, 128), precision=HIGH, preferred_element_type=F32
    )
    denom = weight_sum + reg_col

    await_bytes(val_r.at[pl.ds(0, N_ORI - 1)], recvs.at[4])
    inserted = jnp.dot(scat[0:ROWS, :], val_r[...].reshape(SLOTS, 128), preferred_element_type=F32)
    mapped = jnp.dot(inserted, interp[...], precision=HIGH, preferred_element_type=F32)
    volume = mapped / denom
    vol[...] = volume
    back = lax.dot_general(
        volume, interp[...], (((1,), (1,)), ((), ())), precision=HIGH, preferred_element_type=F32
    )
    reply = jnp.dot(scat_t[:, 0:ROWS], back.astype(BF16), preferred_element_type=F32)
    rep_s[...] = reply.astype(BF16).reshape(N_ORI, CAP, 128)
    spread(rep_s, rep_r, 5)
    rep_r[me_o] = rep_s[me_o]

    await_bytes(gat.at[pl.ds(0, N_ORI - 1)], gat_send)
    for u in range(4):
        pair_copy(u).wait_send()
        await_bytes(z_s.at[u, pl.ds(0, NZ - 1)], z_send.at[u])
    await_bytes(meta_s.at[pl.ds(0, N_ORI - 1)], sends.at[0])
    await_bytes(stat_r.at[pl.ds(0, N_ORI - 1)], sends.at[1])
    await_bytes(mz_s.at[pl.ds(0, N_IMG - 1)], sends.at[2])
    await_bytes(mb_r.at[pl.ds(0, N_ORI - 1)], sends.at[3])
    await_bytes(val_s.at[pl.ds(0, N_ORI - 1)], sends.at[4])

    await_bytes(rep_r.at[pl.ds(0, N_ORI - 1)], recvs.at[5])
    picked = jnp.dot(oh_t[...], rep_r[...].reshape(SLOTS, 128), preferred_element_type=F32)
    for u in range(4):
        for q in range(4):
            res[q * 32 + u * 8 : q * 32 + u * 8 + 8, :] = picked[u * 32 + q * 8 : u * 32 + q * 8 + 8, :]
    await_bytes(rep_s.at[pl.ds(0, N_ORI - 1)], sends.at[5])


def shards(images, references, shifts, owners, slot_rows, interpolation, regularizer):
    vmem = pl.BlockSpec(memory_space=pltpu.VMEM)
    anywhere = pl.BlockSpec(memory_space=pl.ANY)
    volume, resampled = pl.pallas_call(
        kernel,
        out_shape=(jax.ShapeDtypeStruct((ROWS, 128), F32), jax.ShapeDtypeStruct((128, 128), F32)),
        in_specs=[anywhere] * 7,
        out_specs=(vmem, vmem),
        scratch_shapes=[
            pltpu.VMEM((2, COEF), BF16),
            pltpu.VMEM((16, COEF), BF16),
            pltpu.VMEM((2, SHIFTS), F32),
            pltpu.VMEM((1, 128), jnp.int32),
            pltpu.VMEM((1, 128), jnp.int32),
            pltpu.VMEM((128, 128), F32),
            pltpu.VMEM((1, ROWS), F32),
            pltpu.VMEM((N_ORI, 8, QUART), BF16),
            pltpu.VMEM((768, QUART), BF16),
            pltpu.VMEM((2, SHIFTS, QUART), F32),
            pltpu.VMEM((2, SHIFTS, QUART), F32),
            pltpu.VMEM((768, 256), F32),
            pltpu.VMEM((768, 256), BF16),
            pltpu.VMEM((4, N_IMG, 32, 128), F32),
            pltpu.VMEM((4, 32, 128), F32),
            pltpu.VMEM((4, NZ, 32, 128), BF16),
            pltpu.VMEM((4, NZ, 32, 128), BF16),
            pltpu.VMEM((4, NZ, 32, 128), BF16),
            pltpu.VMEM((4, NZ, 32, 128), BF16),
            pltpu.VMEM((N_ORI, 1, 128), F32),
            pltpu.VMEM((N_ORI, 1, 128), F32),
            pltpu.VMEM((1, 1, 256), F32),
            pltpu.VMEM((N_ORI, 1, 256), F32),
            pltpu.VMEM((N_IMG, 1, 128), F32),
            pltpu.VMEM((N_IMG, 1, 128), F32),
            pltpu.VMEM((1, 1, 128), F32),
            pltpu.VMEM((N_ORI, 1, 128), F32),
            pltpu.VMEM((N_ORI, CAP, 128), BF16),
            pltpu.VMEM((N_ORI, CAP, 128), BF16),
            pltpu.VMEM((N_ORI, CAP, 128), BF16),
            pltpu.VMEM((N_ORI, CAP, 128), BF16),
            pltpu.VMEM((SLOTS, 128), BF16),
            pltpu.VMEM((128, SLOTS), BF16),
            pltpu.VMEM((128, SLOTS), BF16),
            pltpu.VMEM((SLOTS, 128), BF16),
            pltpu.VMEM((128, N_ORI), F32),
            pltpu.SemaphoreType.DMA((7,)),
            pltpu.SemaphoreType.DMA,
            pltpu.SemaphoreType.DMA((len(gather_plan()),)),
            pltpu.SemaphoreType.DMA((4,)),
            pltpu.SemaphoreType.DMA((4,)),
            pltpu.SemaphoreType.DMA((4,)),
            pltpu.SemaphoreType.DMA((4,)),
            pltpu.SemaphoreType.DMA((6,)),
            pltpu.SemaphoreType.DMA((6,)),
            pltpu.SemaphoreType.REGULAR((4, 2)),
        ],
        compiler_params=pltpu.CompilerParams(
            collective_id=0, has_side_effects=True, vmem_limit_bytes=60 * 1024 * 1024
        ),
    )(
        images,
        references,
        shifts.T,
        owners.reshape(1, 128),
        slot_rows.reshape(1, 128),
        interpolation,
        regularizer.reshape(1, ROWS),
    )
    return (volume, resampled.reshape(1, COEF))


def solution(mesh):
    in_specs = (
        P(("img", "ori"), None),
        P("ori", None),
        P(),
        P(("ori", "img"), None),
        P(("ori", "img")),
        P(("ori", "img"), None),
        P(("ori", "img")),
    )
    out_specs = (P(("ori", "img"), None), P(("ori", "img"), None))
    return jax.shard_map(shards, mesh=mesh, in_specs=in_specs, out_specs=out_specs, check_vma=False)
```

time: 79.8 us -> 70.9 us (0.89)
  the two profiles are of different devices: /device:TPU:16 before, /device:TPU:8 now
where the time goes in v2:
time: 70.9 us; the launch traced here: 70.7 us
  Pallas kernels  68 us (96%)
  local copies, waits for them, and re-layouts  2.04 us (3%)
    pallas_call x1, Pallas kernels, shards(): pl.pallas_call(kernel, out_shape=(jax.ShapeDtypeStruct((ROWS, 128), F32),...  68 us
    unnamed x4, local copies, waits for them, and re-layouts  2.04 us

profile of v2, /device:TPU:8, one launch (start us, length us, event | category | flops | bytes accessed | tf_op | source)
XLA Modules:
  0.0 70.7 jit_solution(6037467604222509418)
XLA Ops:
  0.6 68.0 %shard_map.86 = (f32[64,128]{1,0:T(8,128)}, f32[128,128]{1,0:T(8,128)}) custom-call(bf16[2,16384]{1,0:T(2,128)(2,1)} %images_h.1, bf16[16,16384]{1,0:T(8,128)(2,1)} %refs_h.1, f32[2,12]{1,0:T(2,128)} %bitcast.6, s32[1,128]{1,0:T(1,128)} %bitcast.7, s32[1,128]{1,0:T(1,128)} %bitcast.8, f32[128,128]{1,0:T(8,128)} %interp_h.1, f32[1,64]{1,0:T(1,128)} %bitcast.9), custom_call_target="tpu_custom_call" | custom-call | tf_op jit(solution)/shard_map/pallas_call | solution.py:415
  68.6 0.0 copy-start
  68.7 1.4 %copy.11 = f32[64,128]{1,0:T(8,128)} copy(f32[64,128]{1,0:T(8,128)} %get-tuple-element.8) | data formatting | bytes 65536
  70.1 0.0 copy-done
  70.1 0.6 copy.12
Async XLA Ops:
  68.6 1.4 %copy-start = (f32[128,128]{1,0:T(8,128)S(1)}, f32[128,128]{1,0:T(8,128)}, u32[]{:S(2)}) copy-start(f32[128,128]{1,0:T(8,128)} %get-tuple-element.5) | copy-start | bytes 196612

commit v3 on v2

--- a/solution.py
+++ b/solution.py
@@ -74,15 +74,19 @@
     return plan
 
 
+def row(half, s, part):
+    return ((half * SHIFTS + s) * 2 + part) * 16
+
+
 def iota(shape, dim):
     return lax.broadcasted_iota(jnp.int32, shape, dim)
 
 
 def kernel(
     images_h, refs_h, shifts_h, owners_h, rows_h, interp_h, reg_h,
-    vol, res,
+    out,
     images, refs, shifts, owners, slot_rows, interp, reg,
-    gat, rot, cos_t, sin_t, acc, wts, part, own_tot, pair_s, pair_r, z_s, z_r,
+    gat, rot, cos_t, sin_t, acc, wts, part, own_tot, pair_s, pair_r, z_s, z_r, relay_r,
     meta_s, meta_r, stat_s, stat_r, mz_s, mz_r, mb_s, mb_r, val_s, val_r, rep_s, rep_r,
     oh, oh_t, scat, scat_t, cnt,
     loc_sem, gat_send, gat_recv, pair_send, pair_recv, z_send, z_recv, sends, recvs, token,
@@ -147,12 +151,9 @@
             imag = refs[:, (2 + half) * QUART + col : (2 + half) * QUART + col + 256].astype(F32)
             for s in range(SHIFTS):
                 cs, sn = cos_t[half, s : s + 1, col : col + 256], sin_t[half, s : s + 1, col : col + 256]
-                rot[half * 192 + s * 16 : half * 192 + s * 16 + 16, col : col + 256] = (
-                    real * cs - imag * sn
-                ).astype(BF16)
-                rot[(2 + half) * 192 + s * 16 : (2 + half) * 192 + s * 16 + 16, col : col + 256] = (
-                    real * sn + imag * cs
-                ).astype(BF16)
+                r = row(half, s, 0)
+                rot[r : r + 16, col : col + 256] = (real * cs - imag * sn).astype(BF16)
+                rot[r + 16 : r + 32, col : col + 256] = (real * sn + imag * cs).astype(BF16)
 
     def routing(step):
         loads[3].wait()
@@ -197,17 +198,20 @@
             device_id={"ori": to}, device_id_type=MESH,
         )
 
+    xs = [lax.rem(x + d, NX) * NY for d in range(NX)]
+    ys = [lax.rem(y + d, NY) for d in range(NY)]
+    others = sorted(
+        ((a, b) for a in range(NX) for b in range(NY) if a or b), key=lambda p: -min(p[0], NX - p[0]) - min(p[1], NY - p[1])
+    )
+
     def spread(send_ref, recv_ref, which):
-        def one(p, carry):
-            to = lax.rem(me_o + p, N_ORI)
+        for a, b in others:
+            to = xs[a] + ys[b]
             src = send_ref.at[0] if send_ref.shape[0] == 1 else send_ref.at[to]
             pltpu.make_async_remote_copy(
                 src_ref=src, dst_ref=recv_ref.at[me_o], send_sem=sends.at[which], recv_sem=recvs.at[which],
                 device_id={"ori": to}, device_id_type=MESH,
             ).start()
-            return carry
-
-        lax.fori_loop(1, N_ORI, one, 0)
 
     def await_bytes(ref, sem):
         pltpu.make_async_copy(ref, ref, sem).wait()
@@ -231,25 +235,22 @@
             job(step)
     for job, step in jobs:
         job(step)
-    spread(meta_s, meta_r, 0)
-    meta_r[me_o] = meta_s[me_o]
-
-    def score(step, carry):
-        cols = pl.ds(step * SCORE_COLS if isinstance(step, int) else pl.multiple_of(step * SCORE_COLS, SCORE_COLS), SCORE_COLS)
-        block = gat[:, :, cols].reshape(N_ORI * 8, SCORE_COLS)
-        got = lax.dot_general(rot[:, cols], block, (((1,), (1,)), ((), ())), preferred_element_type=F32)
-        acc[...] = got if isinstance(step, int) else acc[...] + got
-        return carry
-
-    score(0, 0)
-    if QUART > SCORE_COLS:
-        lax.fori_loop(1, QUART // SCORE_COLS, score, 0)
-
-    lane = iota((192, 256), 1)
-    quarter = lane % 8 // 2
-    mine = jnp.zeros((192, 256), F32)
-    for q in range(4):
-        mine = mine + jnp.where(quarter == q, acc[q * 192 : (q + 1) * 192, :], 0.0)
+    for h in range(2):
+        acc[h * 384 : h * 384 + 384, :] = lax.dot_general(
+            rot[h * 384 : h * 384 + 384, :], gat[...].reshape(N_ORI * 8, QUART), (((1,), (1,)), ((), ())),
+            preferred_element_type=F32)
+
+    quarter = iota((16, 256), 1) % 8 // 2
+    places = [(half, im) for half in range(2) for im in range(2)]
+    mine = []
+    for s in range(SHIFTS):
+        mine.append(
+            sum(
+                jnp.where(quarter == 2 * im + half, acc[row(half, s, im) : row(half, s, im) + 16, :], 0.0)
+                for half, im in places
+            )
+        )
+    mine = jnp.concatenate(mine, axis=0)
     left, right = iota((256, 256), 0), iota((256, 256), 1)
     fold = ((left // 8 == right // 8) & (left % 2 == right % 2)).astype(F32)
     scores = jnp.dot(mine, fold, precision=HIGH, preferred_element_type=F32) * (2.0 / math.sqrt(COEF))
@@ -260,6 +261,124 @@
     stat_s[0] = stat
     spread(stat_s, stat_r, 1)
     stat_r[me_o] = stat
+    spread(meta_s, meta_r, 0)
+    meta_r[me_o] = meta_s[me_o]
+    loads[5].wait()
+    loads[6].wait()
+
+    await_bytes(stat_r.at[pl.ds(0, N_ORI - 1)], recvs.at[1])
+    stats = stat_r[...].reshape(N_ORI, 256)
+    even = iota((N_ORI, 256), 1) // 2 % 2 == 0
+    peaks = jnp.where(even, stats, pltpu.roll(stats, 2, 1))
+    totals = jnp.where(even, pltpu.roll(stats, 254, 1), stats)
+    top = jnp.max(peaks, axis=0, keepdims=True)
+    whole = jnp.sum(totals * jnp.exp(peaks - top), axis=0, keepdims=True)
+    weights = expo * (jnp.exp(peak - top) / whole)
+    for s in range(SHIFTS):
+        for half, im in places:
+            r = row(half, s, im)
+            wts[r : r + 16, :] = jnp.where(quarter == 2 * im + half, weights[s * 16 : s * 16 + 16], 0.0).astype(BF16)
+
+    mass16 = weights[0:16]
+    for s in range(1, SHIFTS):
+        mass16 = mass16 + weights[s * 16 : s * 16 + 16]
+    mass16 = jnp.sum(jnp.where(quarter == 0, mass16, 0.0), axis=1, keepdims=True)
+    mass16 = jnp.broadcast_to(mass16, (16, 128))
+    for o in range(N_IMG):
+        mz_s[o] = mass16[o : o + 1, :]
+
+    def send_mass(p, carry):
+        to = lax.rem(me_i + p, N_IMG)
+        pltpu.make_async_remote_copy(
+            src_ref=mz_s.at[to], dst_ref=mz_r.at[me_i], send_sem=sends.at[2], recv_sem=recvs.at[2],
+            device_id={"img": to}, device_id_type=MESH,
+        ).start()
+        return carry
+
+    lax.fori_loop(1, N_IMG, send_mass, 0)
+    mz_r[me_i] = mz_s[me_i]
+
+    def pair_copy(u):
+        return pltpu.make_async_remote_copy(
+            src_ref=pair_s.at[u], dst_ref=pair_r.at[u], send_sem=pair_send.at[u], recv_sem=pair_recv.at[u],
+            device_id={"img": z * 2 + 1 - c}, device_id_type=MESH,
+        )
+
+    def project(u):
+        for v in range(2):
+            col = u * 1024 + v * 512
+            block = gat[:, :, col : col + 512].reshape(N_ORI * 8, 512)
+            for half in range(2):
+                prod = jnp.dot(wts[half * 384 : half * 384 + 384, :], block, preferred_element_type=F32)
+                re = jnp.zeros((16, 512), F32)
+                im = jnp.zeros((16, 512), F32)
+                for s in range(SHIFTS):
+                    cs, sn = cos_t[half, s : s + 1, col : col + 512], sin_t[half, s : s + 1, col : col + 512]
+                    sr = prod[row(0, s, 0) : row(0, s, 0) + 16, :]
+                    si = prod[row(0, s, 1) : row(0, s, 1) + 16, :]
+                    re = re + sr * cs + si * sn
+                    im = im - sr * sn + si * cs
+                for a in range(4):
+                    part[u, :, half * 8 + v * 4 + a, :] = re[:, a * 128 : a * 128 + 128]
+                    part[u, :, (2 + half) * 8 + v * 4 + a, :] = im[:, a * 128 : a * 128 + 128]
+        for k in range(NZ):
+            pair_s[u, k] = part[u, 2 * k + 1 - c].astype(BF16)
+        pair_copy(u).start()
+
+    zs = [lax.rem(z + d, NZ) for d in range(NZ)]
+
+    def chip_sum(u, to):
+        return part[u, 2 * to + c] + pair_r[u, to].astype(F32)
+
+    def z_copy(u, src, dst, dist, sem):
+        return pltpu.make_async_remote_copy(
+            src_ref=src, dst_ref=dst, send_sem=z_send.at[u], recv_sem=sem,
+            device_id={"img": zs[dist % NZ] * 2 + c}, device_id_type=MESH,
+        )
+
+    def first_leg(u):
+        pair_copy(u).wait_recv()
+        own_tot[u] = chip_sum(u, z)
+        if u == 3:
+            for d in (4, 3, 5, 2, 6, 1, 7):
+                z_s[u, d] = chip_sum(u, zs[d]).astype(BF16)
+                z_copy(u, z_s.at[u, d], z_r.at[u, NZ - d], d, z_recv.at[u, 0]).start()
+            return
+        z_s[u, 4] = chip_sum(u, zs[4]).astype(BF16)
+        for way, (far, via, near_by) in enumerate(((3, 1, 1), (5, 7, 7))):
+            z_s[u, far] = chip_sum(u, zs[far]).astype(BF16)
+            half = pl.ds(way * 16, 16)
+            z_copy(u, z_s.at[u, 4, half], relay_r.at[u, 2 + way, half], 2 * via, z_recv.at[u, 3 + way]).start()
+            z_copy(u, z_s.at[u, far], relay_r.at[u, way], via, z_recv.at[u, 1 + way]).start()
+            z_s[u, near_by] = chip_sum(u, zs[near_by]).astype(BF16)
+        for near_by in (1, 7):
+            z_copy(u, z_s.at[u, near_by], z_r.at[u, NZ - near_by], near_by, z_recv.at[u, 0]).start()
+
+    def second_leg(u):
+        for way, (to, other) in enumerate(((2, 16), (6, 0))):
+            await_bytes(relay_r.at[u, way], z_recv.at[u, 1 + way])
+            half = pl.ds(way * 16, 16)
+            await_bytes(relay_r.at[u, 2 + way, half], z_recv.at[u, 3 + way])
+            total = chip_sum(u, zs[to]) + relay_r[u, way].astype(F32)
+            far = relay_r[u, 2 + way, way * 16 : way * 16 + 16, :].astype(F32)
+            zero = jnp.zeros((16, 128), F32)
+            total = total + jnp.concatenate([zero, far] if way else [far, zero], axis=0)
+            z_s[u, to] = total.astype(BF16)
+            z_copy(u, z_s.at[u, to], z_r.at[u, NZ - to], to, z_recv.at[u, 0]).start()
+
+    project(0)
+    for u in range(1, 4):
+        project(u)
+        first_leg(u - 1)
+    first_leg(3)
+    for u in range(3):
+        second_leg(u)
+
+    await_bytes(mz_r.at[pl.ds(0, N_IMG - 1)], recvs.at[2])
+    mass_all = jnp.sum(mz_r[...].reshape(N_IMG, 128), axis=0, keepdims=True)
+    mb_s[0] = mass_all
+    spread(mb_s, mb_r, 3)
+    mb_r[me_o] = mass_all
 
     await_bytes(meta_r.at[pl.ds(0, N_ORI - 1)], recvs.at[0])
     rep = (iota((SLOTS, N_ORI), 0) // CAP == iota((SLOTS, N_ORI), 1)).astype(BF16)
@@ -269,102 +388,17 @@
     scat_t[...] = hot.astype(BF16)
     scat[...] = jnp.transpose(hot).astype(BF16)
     cnt[...] = jnp.dot(scat[...], rep, preferred_element_type=F32)
-    loads[6].wait()
     reg_col = jnp.sum(
         jnp.where(iota((ROWS, ROWS), 0) == iota((ROWS, ROWS), 1), reg[...], 0.0), axis=1, keepdims=True
     )
 
-    loads[5].wait()
-    await_bytes(stat_r.at[pl.ds(0, N_ORI - 1)], recvs.at[1])
-    stats = stat_r[...].reshape(N_ORI, 256)
-    even = iota((N_ORI, 256), 1) // 2 % 2 == 0
-    peaks = jnp.where(even, stats, pltpu.roll(stats, 2, 1))
-    totals = jnp.where(even, pltpu.roll(stats, 254, 1), stats)
-    top = jnp.max(peaks, axis=0, keepdims=True)
-    whole = jnp.sum(totals * jnp.exp(peaks - top), axis=0, keepdims=True)
-    weights = expo * (jnp.exp(peak - top) / whole)
-    for q in range(4):
-        wts[q * 192 : (q + 1) * 192, :] = jnp.where(quarter == q, weights, 0.0).astype(BF16)
-
-    mass = jnp.sum(jnp.where(quarter == 0, weights, 0.0), axis=1, keepdims=True)
-    mass16 = mass[0:16]
-    for s in range(1, SHIFTS):
-        mass16 = mass16 + mass[s * 16 : s * 16 + 16]
-    mass16 = jnp.broadcast_to(mass16, (16, 128))
-    for o in range(N_IMG):
-        mz_s[o] = mass16[o : o + 1, :]
-
-    def send_mass(p, carry):
-        to = lax.rem(me_i + p, N_IMG)
-        pltpu.make_async_remote_copy(
-            src_ref=mz_s.at[to], dst_ref=mz_r.at[me_i], send_sem=sends.at[2], recv_sem=recvs.at[2],
-            device_id={"img": to}, device_id_type=MESH,
-        ).start()
-        return carry
-
-    lax.fori_loop(1, N_IMG, send_mass, 0)
-    mz_r[me_i] = mz_s[me_i]
-
-    def pair_copy(u):
-        return pltpu.make_async_remote_copy(
-            src_ref=pair_s.at[u], dst_ref=pair_r.at[u], send_sem=pair_send.at[u], recv_sem=pair_recv.at[u],
-            device_id={"img": z * 2 + 1 - c}, device_id_type=MESH,
-        )
-
-    def project(u, carry):
-        for v in range(4):
-            cols = pl.ds(pl.multiple_of(u * 1024 + v * 256, 256), 256)
-            block = gat[:, :, cols].reshape(N_ORI * 8, 256)
-            prod = jnp.dot(wts[...], block, preferred_element_type=F32)
-            for half in range(2):
-                re = jnp.zeros((16, 256), F32)
-                im = jnp.zeros((16, 256), F32)
-                for s in range(SHIFTS):
-                    cs, sn = cos_t[half, s : s + 1, cols], sin_t[half, s : s + 1, cols]
-                    sr = prod[half * 192 + s * 16 : half * 192 + s * 16 + 16, :]
-                    si = prod[(2 + half) * 192 + s * 16 : (2 + half) * 192 + s * 16 + 16, :]
-                    re = re + sr * cs + si * sn
-                    im = im - sr * sn + si * cs
-                for a in range(2):
-                    part[u, :, half * 8 + v * 2 + a, :] = re[:, a * 128 : a * 128 + 128]
-                    part[u, :, (2 + half) * 8 + v * 2 + a, :] = im[:, a * 128 : a * 128 + 128]
-        for k in range(NZ):
-            pair_s[u, k] = part[u, 2 * k + 1 - c].astype(BF16)
-        pair_copy(u).start()
-        return carry
-
-    def reduce_pair(u):
-        pair_copy(u).wait_recv()
-        own_tot[u] = part[u, 2 * z + c] + pair_r[u, z].astype(F32)
-        for p in (4, 3, 5, 2, 6, 1, 7):
-            to = lax.rem(z + p, NZ)
-            z_s[u, to] = (part[u, 2 * to + c] + pair_r[u, to].astype(F32)).astype(BF16)
-            pltpu.make_async_remote_copy(
-                src_ref=z_s.at[u, to], dst_ref=z_r.at[u, z], send_sem=z_send.at[u], recv_sem=z_recv.at[u],
-                device_id={"img": to * 2 + c}, device_id_type=MESH,
-            ).start()
-
-    def project_and_reduce(u, carry):
-        project(u, 0)
-        reduce_pair(u - 1)
-        return carry
-
-    project(0, 0)
-    lax.fori_loop(1, 4, project_and_reduce, 0)
-    reduce_pair(3)
-
-    await_bytes(mz_r.at[pl.ds(0, N_IMG - 1)], recvs.at[2])
-    mass_all = jnp.sum(mz_r[...].reshape(N_IMG, 128), axis=0, keepdims=True)
-    mb_s[0] = mass_all
-    spread(mb_s, mb_r, 3)
-    mb_r[me_o] = mass_all
-
     sums = []
     for u in range(4):
-        await_bytes(z_r.at[u, pl.ds(0, NZ - 1)], z_recv.at[u])
+        sources = (1, 2, 6, 7) if u < 3 else range(1, NZ)
+        await_bytes(z_r.at[u, pl.ds(0, len(sources))], z_recv.at[u, 0])
         tot = own_tot[u]
-        for p in range(1, NZ):
-            tot = tot + z_r[u, lax.rem(z + p, NZ)].astype(F32)
+        for d in sources:
+            tot = tot + z_r[u, d].astype(F32)
         sums.append(tot)
     segments = jnp.concatenate(sums, axis=0).astype(BF16)
 
@@ -382,7 +416,7 @@
     inserted = jnp.dot(scat[0:ROWS, :], val_r[...].reshape(SLOTS, 128), preferred_element_type=F32)
     mapped = jnp.dot(inserted, interp[...], precision=HIGH, preferred_element_type=F32)
     volume = mapped / denom
-    vol[...] = volume
+    out[0:ROWS, :] = volume
     back = lax.dot_general(
         volume, interp[...], (((1,), (1,)), ((), ())), precision=HIGH, preferred_element_type=F32
     )
@@ -405,18 +439,24 @@
     picked = jnp.dot(oh_t[...], rep_r[...].reshape(SLOTS, 128), preferred_element_type=F32)
     for u in range(4):
         for q in range(4):
-            res[q * 32 + u * 8 : q * 32 + u * 8 + 8, :] = picked[u * 32 + q * 8 : u * 32 + q * 8 + 8, :]
+            to = ROWS + q * 32 + u * 8
+            out[to : to + 8, :] = picked[u * 32 + q * 8 : u * 32 + q * 8 + 8, :]
     await_bytes(rep_s.at[pl.ds(0, N_ORI - 1)], sends.at[5])
+
+
+def hand_over(both, vol, res):
+    vol[...] = both[0:ROWS, :]
+    res[...] = both[ROWS : ROWS + 128, :]
 
 
 def shards(images, references, shifts, owners, slot_rows, interpolation, regularizer):
     vmem = pl.BlockSpec(memory_space=pltpu.VMEM)
     anywhere = pl.BlockSpec(memory_space=pl.ANY)
-    volume, resampled = pl.pallas_call(
+    both = pl.pallas_call(
         kernel,
-        out_shape=(jax.ShapeDtypeStruct((ROWS, 128), F32), jax.ShapeDtypeStruct((128, 128), F32)),
+        out_shape=jax.ShapeDtypeStruct((ROWS + 128, 128), F32),
         in_specs=[anywhere] * 7,
-        out_specs=(vmem, vmem),
+        out_specs=vmem,
         scratch_shapes=[
             pltpu.VMEM((2, COEF), BF16),
             pltpu.VMEM((16, COEF), BF16),
@@ -437,6 +477,7 @@
             pltpu.VMEM((4, NZ, 32, 128), BF16),
             pltpu.VMEM((4, NZ, 32, 128), BF16),
             pltpu.VMEM((4, NZ, 32, 128), BF16),
+            pltpu.VMEM((3, 4, 32, 128), BF16),
             pltpu.VMEM((N_ORI, 1, 128), F32),
             pltpu.VMEM((N_ORI, 1, 128), F32),
             pltpu.VMEM((1, 1, 256), F32),
@@ -460,7 +501,7 @@
             pltpu.SemaphoreType.DMA((4,)),
             pltpu.SemaphoreType.DMA((4,)),
             pltpu.SemaphoreType.DMA((4,)),
-            pltpu.SemaphoreType.DMA((4,)),
+            pltpu.SemaphoreType.DMA((4, 5)),
             pltpu.SemaphoreType.DMA((6,)),
             pltpu.SemaphoreType.DMA((6,)),
             pltpu.SemaphoreType.REGULAR((4, 2)),
@@ -477,6 +518,12 @@
         interpolation,
         regularizer.reshape(1, ROWS),
     )
+    volume, resampled = pl.pallas_call(
+        hand_over,
+        out_shape=(jax.ShapeDtypeStruct((ROWS, 128), F32), jax.ShapeDtypeStruct((128, 128), F32)),
+        in_specs=[vmem],
+        out_specs=(vmem, vmem),
+    )(both)
     return (volume, resampled.reshape(1, COEF))
 
 

time: 70.9 us -> 67 us (0.945)
  local copies, waits for them, and re-layouts: 2.04 us -> 0 us
  Pallas kernels: 68 us -> 66.2 us
    unnamed x4 -> x0, local copies, waits for them, and re-layouts: 2.04 us -> none
    pallas_call x1 -> x2, Pallas kernels: 68 us -> 66.2 us  [the longest x1 64.6 us: shards(): pl.pallas_call(kernel, out_shape=jax.ShapeDtypeStruct((ROWS + 128, 128),...]
where the time goes in v3:
time: 67 us; the launch traced here: 66.8 us
  Pallas kernels  66.2 us (99%)
    pallas_call x1, Pallas kernels, shards(): pl.pallas_call(kernel, out_shape=jax.ShapeDtypeStruct((ROWS + 128, 128),...  64.6 us
    pallas_call x1, Pallas kernels, shards(): pl.pallas_call(hand_over, out_shape=(jax.ShapeDtypeStruct((ROWS, 128), F3...  1.54 us

profile of v3, /device:TPU:8, one launch (start us, length us, event | category | flops | bytes accessed | tf_op | source)
XLA Modules:
  0.0 66.8 jit_solution(613903204473478122)
XLA Ops:
  0.6 64.6 %shard_map.86.both = f32[192,128]{1,0:T(8,128)} custom-call(bf16[2,16384]{1,0:T(2,128)(2,1)} %images_h.1, bf16[16,16384]{1,0:T(8,128)(2,1)} %refs_h.1, f32[2,12]{1,0:T(2,128)} %bitcast.5, s32[1,128]{1,0:T(1,128)} %bitcast.6, s32[1,128]{1,0:T(1,128)} %bitcast.7, f32[128,128]{1,0:T(8,128)} %interp_h.1, f32[1,64]{1,0:T(1,128)} %bitcast.8), custom_call_target="tpu_custom_call" | custom-call | tf_op jit(solution)/shard_map/pallas_call | solution.py:455
  65.3 1.5 %shard_map.87 = (f32[64,128]{1,0:T(8,128)}, f32[128,128]{1,0:T(8,128)}) custom-call(f32[192,128]{1,0:T(8,128)} %shard_map.86.both), custom_call_target="tpu_custom_call" | custom-call | tf_op jit(solution)/shard_map/pallas_call | solution.py:521

commit v4 on v3

--- a/solution.py
+++ b/solution.py
@@ -222,7 +222,7 @@
     jobs[10:10] = [(pass_token, 2)]
     jobs[14:14] = [(pass_token, 3)]
     jobs += [(pass_token, 4), (routing, 0)]
-    due = [2 + i * (len(plan) - 8) // len(jobs) for i in range(len(jobs))]
+    due = [1] * 8 + [5 + i * (len(plan) - 12) // (len(jobs) - 8) for i in range(len(jobs) - 8)]
     for i, (block, hops) in enumerate(plan):
         dx, dy = block[3:5]
         if dx or dy:
@@ -279,25 +279,6 @@
             r = row(half, s, im)
             wts[r : r + 16, :] = jnp.where(quarter == 2 * im + half, weights[s * 16 : s * 16 + 16], 0.0).astype(BF16)
 
-    mass16 = weights[0:16]
-    for s in range(1, SHIFTS):
-        mass16 = mass16 + weights[s * 16 : s * 16 + 16]
-    mass16 = jnp.sum(jnp.where(quarter == 0, mass16, 0.0), axis=1, keepdims=True)
-    mass16 = jnp.broadcast_to(mass16, (16, 128))
-    for o in range(N_IMG):
-        mz_s[o] = mass16[o : o + 1, :]
-
-    def send_mass(p, carry):
-        to = lax.rem(me_i + p, N_IMG)
-        pltpu.make_async_remote_copy(
-            src_ref=mz_s.at[to], dst_ref=mz_r.at[me_i], send_sem=sends.at[2], recv_sem=recvs.at[2],
-            device_id={"img": to}, device_id_type=MESH,
-        ).start()
-        return carry
-
-    lax.fori_loop(1, N_IMG, send_mass, 0)
-    mz_r[me_i] = mz_s[me_i]
-
     def pair_copy(u):
         return pltpu.make_async_remote_copy(
             src_ref=pair_s.at[u], dst_ref=pair_r.at[u], send_sem=pair_send.at[u], recv_sem=pair_recv.at[u],
@@ -305,22 +286,24 @@
         )
 
     def project(u):
-        for v in range(2):
-            col = u * 1024 + v * 512
-            block = gat[:, :, col : col + 512].reshape(N_ORI * 8, 512)
-            for half in range(2):
+        for half in range(2):
+            res, ims = [], []
+            for v in range(1024 // 512):
+                cols = slice(u * 1024 + v * 512, u * 1024 + v * 512 + 512)
+                block = gat[:, :, cols].reshape(N_ORI * 8, 512)
                 prod = jnp.dot(wts[half * 384 : half * 384 + 384, :], block, preferred_element_type=F32)
                 re = jnp.zeros((16, 512), F32)
                 im = jnp.zeros((16, 512), F32)
                 for s in range(SHIFTS):
-                    cs, sn = cos_t[half, s : s + 1, col : col + 512], sin_t[half, s : s + 1, col : col + 512]
-                    sr = prod[row(0, s, 0) : row(0, s, 0) + 16, :]
-                    si = prod[row(0, s, 1) : row(0, s, 1) + 16, :]
+                    cs, sn = cos_t[half, s : s + 1, cols], sin_t[half, s : s + 1, cols]
+                    sr = prod[s * 32 : s * 32 + 16, :]
+                    si = prod[s * 32 + 16 : s * 32 + 32, :]
                     re = re + sr * cs + si * sn
                     im = im - sr * sn + si * cs
-                for a in range(4):
-                    part[u, :, half * 8 + v * 4 + a, :] = re[:, a * 128 : a * 128 + 128]
-                    part[u, :, (2 + half) * 8 + v * 4 + a, :] = im[:, a * 128 : a * 128 + 128]
+                res.append(re)
+                ims.append(im)
+            for first, sums in ((half * 8, res), (16 + half * 8, ims)):
+                part[u, :, first : first + 8, :] = jnp.concatenate(sums, axis=1).reshape(16, 8, 128)
         for k in range(NZ):
             pair_s[u, k] = part[u, 2 * k + 1 - c].astype(BF16)
         pair_copy(u).start()
@@ -367,6 +350,26 @@
             z_copy(u, z_s.at[u, to], z_r.at[u, NZ - to], to, z_recv.at[u, 0]).start()
 
     project(0)
+
+    mass16 = weights[0:16]
+    for s in range(1, SHIFTS):
+        mass16 = mass16 + weights[s * 16 : s * 16 + 16]
+    mass16 = jnp.sum(jnp.where(quarter == 0, mass16, 0.0), axis=1, keepdims=True)
+    mass16 = jnp.broadcast_to(mass16, (16, 128))
+    for o in range(N_IMG):
+        mz_s[o] = mass16[o : o + 1, :]
+
+    def send_mass(p, carry):
+        to = lax.rem(me_i + p, N_IMG)
+        pltpu.make_async_remote_copy(
+            src_ref=mz_s.at[to], dst_ref=mz_r.at[me_i], send_sem=sends.at[2], recv_sem=recvs.at[2],
+            device_id={"img": to}, device_id_type=MESH,
+        ).start()
+        return carry
+
+    lax.fori_loop(1, N_IMG, send_mass, 0)
+    mz_r[me_i] = mz_s[me_i]
+
     for u in range(1, 4):
         project(u)
         first_leg(u - 1)
@@ -392,6 +395,10 @@
         jnp.where(iota((ROWS, ROWS), 0) == iota((ROWS, ROWS), 1), reg[...], 0.0), axis=1, keepdims=True
     )
 
+    gram = lax.dot_general(
+        interp[...], interp[...], (((1,), (1,)), ((), ())), precision=HIGH, preferred_element_type=F32
+    )
+
     sums = []
     for u in range(4):
         sources = (1, 2, 6, 7) if u < 3 else range(1, NZ)
@@ -410,20 +417,16 @@
     weight_sum = jnp.dot(
         cnt[0:ROWS, :], mb_r[...].reshape(N_ORI, 128), precision=HIGH, preferred_element_type=F32
     )
-    denom = weight_sum + reg_col
+    inverse = 1.0 / (weight_sum + reg_col)
 
     await_bytes(val_r.at[pl.ds(0, N_ORI - 1)], recvs.at[4])
     inserted = jnp.dot(scat[0:ROWS, :], val_r[...].reshape(SLOTS, 128), preferred_element_type=F32)
-    mapped = jnp.dot(inserted, interp[...], precision=HIGH, preferred_element_type=F32)
-    volume = mapped / denom
-    out[0:ROWS, :] = volume
-    back = lax.dot_general(
-        volume, interp[...], (((1,), (1,)), ((), ())), precision=HIGH, preferred_element_type=F32
-    )
+    back = jnp.dot(inserted, gram, precision=HIGH, preferred_element_type=F32) * inverse
     reply = jnp.dot(scat_t[:, 0:ROWS], back.astype(BF16), preferred_element_type=F32)
     rep_s[...] = reply.astype(BF16).reshape(N_ORI, CAP, 128)
     spread(rep_s, rep_r, 5)
     rep_r[me_o] = rep_s[me_o]
+    out[0:ROWS, :] = jnp.dot(inserted, interp[...], precision=HIGH, preferred_element_type=F32) * inverse
 
     await_bytes(gat.at[pl.ds(0, N_ORI - 1)], gat_send)
     for u in range(4):
@@ -452,6 +455,15 @@
 def shards(images, references, shifts, owners, slot_rows, interpolation, regularizer):
     vmem = pl.BlockSpec(memory_space=pltpu.VMEM)
     anywhere = pl.BlockSpec(memory_space=pl.ANY)
+    operands = (
+        images,
+        references,
+        shifts.T,
+        owners.reshape(1, 128),
+        slot_rows.reshape(1, 128),
+        interpolation,
+        regularizer.reshape(1, ROWS),
+    )
     both = pl.pallas_call(
         kernel,
         out_shape=jax.ShapeDtypeStruct((ROWS + 128, 128), F32),
@@ -507,22 +519,15 @@
             pltpu.SemaphoreType.REGULAR((4, 2)),
         ],
         compiler_params=pltpu.CompilerParams(
-            collective_id=0, has_side_effects=True, vmem_limit_bytes=60 * 1024 * 1024
+            collective_id=0, has_side_effects=True, vmem_limit_bytes=40 * 1024 * 1024
         ),
-    )(
-        images,
-        references,
-        shifts.T,
-        owners.reshape(1, 128),
-        slot_rows.reshape(1, 128),
-        interpolation,
-        regularizer.reshape(1, ROWS),
-    )
+    )(*(pltpu.with_memory_space_constraint(operand, pltpu.HBM) for operand in operands))
     volume, resampled = pl.pallas_call(
         hand_over,
         out_shape=(jax.ShapeDtypeStruct((ROWS, 128), F32), jax.ShapeDtypeStruct((128, 128), F32)),
         in_specs=[vmem],
         out_specs=(vmem, vmem),
+        compiler_params=pltpu.CompilerParams(vmem_limit_bytes=4 * 1024 * 1024),
     )(both)
     return (volume, resampled.reshape(1, COEF))
 

time: 67 us -> 64.9 us (0.969)
  Pallas kernels: 66.2 us -> 64.1 us
    pallas_call x1, Pallas kernels: 64.6 us -> 63.5 us  [shards(): pl.pallas_call(kernel, out_shape=jax.ShapeDtypeStruct((ROWS + 128, 128),...]
    pallas_call x1, Pallas kernels: 1.54 us -> 0.65 us  [shards(): pl.pallas_call(hand_over, out_shape=(jax.ShapeDtypeStruct((ROWS, 128), F3...]
where the time goes in v4:
time: 64.9 us; the launch traced here: 64.8 us
  Pallas kernels  64.1 us (99%)
    pallas_call x1, Pallas kernels, shards(): pl.pallas_call(kernel, out_shape=jax.ShapeDtypeStruct((ROWS + 128, 128),...  63.5 us

profile of v4, /device:TPU:8, one launch (start us, length us, event | category | flops | bytes accessed | tf_op | source)
XLA Modules:
  0.0 64.8 jit_solution(362285432048716988)
XLA Ops:
  0.6 63.5 %shard_map.86.both = f32[192,128]{1,0:T(8,128)S(1)} custom-call(bf16[2,16384]{1,0:T(2,128)(2,1)} %images_h.1, bf16[16,16384]{1,0:T(8,128)(2,1)} %refs_h.1, f32[2,12]{1,0:T(2,128)} %bitcast.5, s32[1,128]{1,0:T(1,128)} %bitcast.6, s32[1,128]{1,0:T(1,128)} %bitcast.7, f32[128,128]{1,0:T(8,128)} %interp_h.1, f32[1,64]{1,0:T(1,128)} %bitcast.8), custom_call_target="tpu_custom_call" | custom-call | tf_op jit(solution)/shard_map/pallas_call | solution.py:467
  64.1 0.6 %shard_map.87 = (f32[64,128]{1,0:T(8,128)}, f32[128,128]{1,0:T(8,128)}) custom-call(f32[192,128]{1,0:T(8,128)S(1)} %shard_map.86.both), custom_call_target="tpu_custom_call" | custom-call | tf_op jit(solution)/shard_map/pallas_call | solution.py:525

commit v5 on v4

--- a/solution.py
+++ b/solution.py
@@ -350,6 +350,12 @@
             z_copy(u, z_s.at[u, to], z_r.at[u, NZ - to], to, z_recv.at[u, 0]).start()
 
     project(0)
+    project(1)
+    project(2)
+    first_leg(0)
+    project(3)
+    first_leg(1)
+    first_leg(2)
 
     mass16 = weights[0:16]
     for s in range(1, SHIFTS):
@@ -370,9 +376,6 @@
     lax.fori_loop(1, N_IMG, send_mass, 0)
     mz_r[me_i] = mz_s[me_i]
 
-    for u in range(1, 4):
-        project(u)
-        first_leg(u - 1)
     first_leg(3)
     for u in range(3):
         second_leg(u)

time: 64.9 us -> 64.8 us (level)
  no operation moved by 1% of the time
where the time goes in v5:
time: 64.8 us; the launch traced here: 64.7 us
  Pallas kernels  64 us (99%)
    pallas_call x1, Pallas kernels, shards(): pl.pallas_call(kernel, out_shape=jax.ShapeDtypeStruct((ROWS + 128, 128),...  63.4 us

profile of v5, /device:TPU:8, one launch (start us, length us, event | category | flops | bytes accessed | tf_op | source)
XLA Modules:
  0.0 64.7 jit_solution(5660214491522351169)
XLA Ops:
  0.6 63.4 %shard_map.86.both = f32[192,128]{1,0:T(8,128)S(1)} custom-call(bf16[2,16384]{1,0:T(2,128)(2,1)} %images_h.1, bf16[16,16384]{1,0:T(8,128)(2,1)} %refs_h.1, f32[2,12]{1,0:T(2,128)} %bitcast.5, s32[1,128]{1,0:T(1,128)} %bitcast.6, s32[1,128]{1,0:T(1,128)} %bitcast.7, f32[128,128]{1,0:T(8,128)} %interp_h.1, f32[1,64]{1,0:T(1,128)} %bitcast.8), custom_call_target="tpu_custom_call" | custom-call | tf_op jit(solution)/shard_map/pallas_call | solution.py:470
  64.0 0.6 %shard_map.87 = (f32[64,128]{1,0:T(8,128)}, f32[128,128]{1,0:T(8,128)}) custom-call(f32[192,128]{1,0:T(8,128)S(1)} %shard_map.86.both), custom_call_target="tpu_custom_call" | custom-call | tf_op jit(solution)/shard_map/pallas_call | solution.py:528

commit v6 on v5

--- a/solution.py
+++ b/solution.py
@@ -376,16 +376,6 @@
     lax.fori_loop(1, N_IMG, send_mass, 0)
     mz_r[me_i] = mz_s[me_i]
 
-    first_leg(3)
-    for u in range(3):
-        second_leg(u)
-
-    await_bytes(mz_r.at[pl.ds(0, N_IMG - 1)], recvs.at[2])
-    mass_all = jnp.sum(mz_r[...].reshape(N_IMG, 128), axis=0, keepdims=True)
-    mb_s[0] = mass_all
-    spread(mb_s, mb_r, 3)
-    mb_r[me_o] = mass_all
-
     await_bytes(meta_r.at[pl.ds(0, N_ORI - 1)], recvs.at[0])
     rep = (iota((SLOTS, N_ORI), 0) // CAP == iota((SLOTS, N_ORI), 1)).astype(BF16)
     rid = jnp.dot(rep, meta_r[...].reshape(N_ORI, 128).astype(BF16), preferred_element_type=F32)
@@ -401,6 +391,16 @@
     gram = lax.dot_general(
         interp[...], interp[...], (((1,), (1,)), ((), ())), precision=HIGH, preferred_element_type=F32
     )
+
+    first_leg(3)
+    for u in range(3):
+        second_leg(u)
+
+    await_bytes(mz_r.at[pl.ds(0, N_IMG - 1)], recvs.at[2])
+    mass_all = jnp.sum(mz_r[...].reshape(N_IMG, 128), axis=0, keepdims=True)
+    mb_s[0] = mass_all
+    spread(mb_s, mb_r, 3)
+    mb_r[me_o] = mass_all
 
     sums = []
     for u in range(4):

time: 64.8 us -> 64.8 us (level)
  the two profiles are of different devices: /device:TPU:8 before, /device:TPU:2 now
where the time goes in v6:
time: 64.8 us; the launch traced here: 64.7 us
  Pallas kernels  64 us (99%)
    pallas_call x1, Pallas kernels, shards(): pl.pallas_call(kernel, out_shape=jax.ShapeDtypeStruct((ROWS + 128, 128),...  63.4 us

profile of v6, /device:TPU:2, one launch (start us, length us, event | category | flops | bytes accessed | tf_op | source)
XLA Modules:
  0.0 64.7 jit_solution(17522239822237929808)
XLA Ops:
  0.6 63.4 %shard_map.86.both = f32[192,128]{1,0:T(8,128)S(1)} custom-call(bf16[2,16384]{1,0:T(2,128)(2,1)} %images_h.1, bf16[16,16384]{1,0:T(8,128)(2,1)} %refs_h.1, f32[2,12]{1,0:T(2,128)} %bitcast.5, s32[1,128]{1,0:T(1,128)} %bitcast.6, s32[1,128]{1,0:T(1,128)} %bitcast.7, f32[128,128]{1,0:T(8,128)} %interp_h.1, f32[1,64]{1,0:T(1,128)} %bitcast.8), custom_call_target="tpu_custom_call" | custom-call | tf_op jit(solution)/shard_map/pallas_call | solution.py:470
  64.0 0.6 %shard_map.87 = (f32[64,128]{1,0:T(8,128)}, f32[128,128]{1,0:T(8,128)}) custom-call(f32[192,128]{1,0:T(8,128)S(1)} %shard_map.86.both), custom_call_target="tpu_custom_call" | custom-call | tf_op jit(solution)/shard_map/pallas_call | solution.py:528
